TPU v7x, 32 devices: a whole 2x2x4 slice. The times are simulated.
32 devices in a mesh: slab: 8 (over z, y), band: 4 (over x, core).
Axes of the slice: x: 2, y: 2, z: 4, core: 2. Of those that a mesh axis runs over, the one named last changes fastest.
Arguments:
- orbitals: float32 [8, 128, 128, 128], P('band', 'slab'), may hold values from -6 to 6
Outputs:
- exchange_out: float32 [8, 128, 128, 128], P('band', 'slab')
All inputs are finite; a program needn't handle non-finite values.
Results may differ from a plain program's by a relative error of at most 0.00013.
Values sent between devices are 32-bit elements; how exact they have to be, the bound alone decides.
No kernel may reach another device: no remote copies, remote signals or barrier semaphores. Data moves between devices by JAX's collectives and lax.ppermute only.
A program may use at most 64 MiB of HBM per device.

v0:
```python
import functools
import math

import jax
import jax.numpy as jnp
from jax import lax
from jax.experimental import pallas as pl
from jax.experimental.pallas import tpu as pltpu
from jax.sharding import Mesh, PartitionSpec as P


screen_width = 0.5
highest = lax.Precision.HIGHEST


def frequency(counter, length):
    return jnp.where(counter < length // 2, counter, counter - length).astype(jnp.float32)


def screened(squared):
    safe_sq = jnp.where(squared > 0, squared, 1.0)
    value = 4.0 * math.pi / safe_sq * (1.0 - jnp.exp(-safe_sq / (4.0 * screen_width**2)))
    return jnp.where(squared > 0, value, math.pi / screen_width**2)


def cas_table(rows, columns, length):
    product = rows[:, None] * columns[None, :] % length
    angles = 2.0 * math.pi / length * product.astype(jnp.float32)
    return jnp.cos(angles) + jnp.sin(angles)


def halves(value):
    high = value.astype(jnp.bfloat16)
    return high, (value - high.astype(jnp.float32)).astype(jnp.bfloat16)


def table_halves(table):
    high = lax.reduce_precision(table, exponent_bits=8, mantissa_bits=7)
    return high.astype(jnp.bfloat16), (table - high).astype(jnp.bfloat16)


def right_table(table):
    high, low = table_halves(table)
    top = jnp.concatenate([high, low], axis=1)
    return jnp.concatenate([top, jnp.concatenate([high, jnp.zeros_like(low)], axis=1)], axis=0)


def left_table(table):
    high, low = table_halves(table)
    top = jnp.concatenate([high, high], axis=1)
    return jnp.concatenate([top, jnp.concatenate([low, jnp.zeros_like(low)], axis=1)], axis=0)


def times_right(value, table):
    width = value.shape[1]
    high, low = halves(value)
    both = jnp.dot(
        jnp.concatenate([high, low], axis=1), table, preferred_element_type=jnp.float32
    )
    return both[:, :width] + both[:, width:]


def times_left(table, value):
    high, low = halves(value)
    both = jnp.dot(
        table, jnp.concatenate([high, low], axis=0), preferred_element_type=jnp.float32
    )
    rows = both.shape[0] // 2
    return both[:rows] + both[rows:]


def spot_of(plane, planes, pieces):
    half, reach = planes // 2, planes // pieces // 2
    return plane % half // reach, plane // half * reach + plane % reach


def pair_at(refs, plane, planes, pieces):
    piece, place = spot_of(plane, planes, pieces)
    return refs[piece][place : place + 2]


def forward_kernel(group, pieces, pairs, left_ref, right_ref, *refs):
    refs, out_refs = refs[:-group], refs[-group:]
    piece, rows, columns = refs[0].shape
    share = rows // group
    planes = piece * pieces
    orbitals = [refs[at : at + pieces] for at in range(0, len(refs), pieces)]
    for which, (first, second) in enumerate(pairs):
        for plane in range(0, planes, 2):
            density = pair_at(orbitals[first], plane, planes, pieces)
            density = density * pair_at(orbitals[second], plane, planes, pieces)
            part = times_right(density.reshape(2 * rows, columns), right_ref[...])
            part = times_left(left_ref[...], jnp.concatenate([part[:rows], part[rows:]], axis=1))
            for offset in range(2):
                lines = part[:, offset * columns : (offset + 1) * columns]
                for chunk in range(group):
                    out_refs[chunk][which, pl.ds(plane + offset, share, stride=planes), :] = lines[
                        chunk * share : (chunk + 1) * share
                    ]


def depth_kernel(planes, group, forth_ref, back_ref, weight_ref, *refs):
    in_refs, out_refs = refs[:group], refs[group:]
    parts = len(out_refs) // group
    reach = planes // parts
    share = in_refs[0].shape[1] // planes
    columns = in_refs[0].shape[2]
    for row in range(0, share, 2):
        value = jnp.concatenate(
            [
                jnp.concatenate(
                    [ref[0, at * planes : (at + 1) * planes, :] for ref in in_refs], axis=0
                )
                for at in (row, row + 1)
            ],
            axis=1,
        )
        value = times_left(forth_ref[...], value) * weight_ref[row // 2]
        value = times_left(back_ref[...], value)
        for offset, at in enumerate((row, row + 1)):
            for place, ref in enumerate(out_refs):
                first = place % group * planes + place // group * reach
                ref[0, at * reach : (at + 1) * reach, :] = value[
                    first : first + reach, offset * columns : (offset + 1) * columns
                ]


def potential_planes(plane, planes, which, left_ref, right_ref, in_refs):
    columns = in_refs[0].shape[2]
    share = in_refs[0].shape[1] // planes
    rows = len(in_refs) * share
    value = jnp.concatenate(
        [
            jnp.concatenate(
                [ref[which, pl.ds(plane + offset, share, stride=planes), :] for ref in in_refs],
                axis=0,
            )
            for offset in range(2)
        ],
        axis=1,
    )
    value = times_left(left_ref[...], value)
    value = jnp.concatenate([value[:, :columns], value[:, columns:]], axis=0)
    return times_right(value, right_ref[...]).reshape(2, rows, columns)


def inverse_kernel(uses, names, pieces, group, begin, left_ref, right_ref, *refs):
    factors, held, targets = names
    in_refs, refs = refs[:group], refs[group:]
    factor_refs = {
        factor: refs[place * pieces : (place + 1) * pieces] for place, factor in enumerate(factors)
    }
    planes = refs[0].shape[0] * pieces
    refs = refs[len(factors) * pieces :]
    held_refs, out_refs = dict(zip(held, refs)), dict(zip(targets, refs[len(held) :]))
    count = refs[-1].shape[0]
    for plane in range(0, count, 2):
        total = {target: held_refs[target][begin + plane : begin + plane + 2] for target in held}
        for which, pairs in enumerate(uses):
            field = potential_planes(plane, count, which, left_ref, right_ref, in_refs)
            for target, factor in pairs:
                term = field * pair_at(factor_refs[factor], begin + plane, planes, pieces)
                total[target] = total[target] - term if target in total else -term
        for target in targets:
            out_refs[target][plane : plane + 2] = total[target]


grant = pltpu.CompilerParams(vmem_limit_bytes=16 * 1024 * 1024)


def whole(shape):
    return pl.BlockSpec(shape, lambda *grid: (0,) * len(shape))


def cost(steps):
    return pl.CostEstimate(flops=steps * 700_000_000, bytes_accessed=steps * 3_000_000, transcendentals=0)


def forward(pairs, known, group, left, right):
    used = sorted({index for pair in pairs for index in pair})
    pieces = len(known[used[0]])
    piece, rows, columns = known[used[0]][0].shape
    chunk = jax.ShapeDtypeStruct((len(pairs), rows // group * piece * pieces, columns), jnp.float32)
    places = [(used.index(first), used.index(second)) for first, second in pairs]
    return pl.pallas_call(
        functools.partial(forward_kernel, group, pieces, places),
        out_shape=[chunk] * group,
        cost_estimate=cost(len(pairs)),
        compiler_params=grant,
        name="forward",
    )(left, right, *[part for index in used for part in known[index]])


def through_depth(values, planes, parts, forth, back, weight):
    count, lines, columns = values[0].shape
    group, reach = len(values), lines // parts

    def block(size):
        return pl.BlockSpec((1, size, columns), lambda step: (step, 0, 0))

    return pl.pallas_call(
        functools.partial(depth_kernel, planes, group),
        grid=(count,),
        in_specs=[whole(forth.shape), whole(back.shape), whole(weight.shape)]
        + [block(lines)] * group,
        out_specs=[block(reach)] * (group * parts),
        out_shape=[jax.ShapeDtypeStruct((count, reach, columns), jnp.float32)] * (group * parts),
        cost_estimate=cost(count),
        compiler_params=grant,
        name="through_depth",
    )(forth, back, weight, *values)


def inverse(values, uses, known, held, begin, left, right):
    factors = sorted({factor for pairs in uses for _, factor in pairs})
    targets = sorted({target for pairs in uses for target, _ in pairs})
    given = [target for target in targets if target in held]
    pieces = len(known[factors[0]])
    _, rows, columns = known[factors[0]][0].shape
    planes = values[0].shape[1] * len(values) // rows
    result = jax.ShapeDtypeStruct((planes, rows, columns), jnp.float32)
    names = (factors, given, targets)
    results = pl.pallas_call(
        functools.partial(inverse_kernel, uses, names, pieces, len(values), begin),
        out_shape=[result] * len(targets),
        cost_estimate=cost(len(uses)),
        compiler_params=grant,
        name="inverse",
    )(
        left,
        right,
        *values,
        *[part for factor in factors for part in known[factor]],
        *[held[target] for target in given],
    )
    return dict(zip(targets, results))


def batch_list(count):
    batches = [[(i, j)] for j in range(count) for i in range(j + 1)]
    batches += [[(i, count + j)] for i in range(count - 1) for j in range(count)]
    return batches + [[(count - 1, count + j) for j in range(count)]]


def schedule(count):
    total = len(batch_list(count))
    own, last = count * (count + 1) // 2, total - 1
    order = ["f0", "d0"] + [f"f{batch}" for batch in range(1, own)] + ["i0"]
    order += [f"d{batch}" for batch in range(1, own)]
    for batch in range(own, last):
        order += [f"f{batch}"] + ([f"i{batch - own + 1}"] if batch - own + 1 < own else [])
    order += [f"i{batch}" for batch in range(last - own + 1, own)]
    order += [f"d{own}", f"f{last}"] + [f"d{batch}" for batch in range(own + 1, last)]
    order += [f"i{batch}" for batch in range(own, last - 1)]
    return order + [f"d{last}", f"i{last - 1}", f"i{last}", f"i{last}b"]


def after(value, *earlier):
    return lax.optimization_barrier((value,) + earlier)[0]


def layered_body(orbitals):
    blocks = lax.axis_size("band")
    inner = lax.axis_size("inner")
    count, planes, rows, columns = orbitals.shape
    piece = planes // blocks
    group = inner * blocks
    depth = planes * inner * blocks
    share = rows // group
    layer = lax.axis_index("layer")
    band = lax.axis_index("band")
    me = lax.axis_index(("inner", "band"))

    counter = jnp.arange(columns, dtype=jnp.int32)
    across = right_table(cas_table(counter, counter, columns))
    counter = jnp.arange(rows, dtype=jnp.int32)
    held_rows = (counter // share ^ me) * share + counter % share
    along_table = cas_table(held_rows, counter, rows)
    along = left_table(along_table)
    along_back = left_table(along_table.T)
    counter = jnp.arange(depth, dtype=jnp.int32)
    source, local = counter // planes ^ me, counter % planes
    slot, offset = spot_of(local, planes, blocks)
    place = (slot ^ layer) * (inner * planes) + source // blocks * planes
    place = place + source % blocks * piece + offset
    depth_table = cas_table(counter, place, depth)
    forth = left_table(depth_table)
    back = left_table(depth_table.T)

    freq_z = 2.0 * math.pi / depth * frequency(counter, depth)
    mine = me * share + jnp.arange(share, dtype=jnp.int32)
    freq_y = 2.0 * math.pi / rows * frequency(mine, rows)
    freq_x = 2.0 * math.pi / columns * frequency(jnp.arange(columns, dtype=jnp.int32), columns)
    squared = (freq_y**2).reshape(share // 2, 1, 2, 1) + (freq_z**2)[None, :, None, None]
    squared = squared + (freq_x**2)[None, None, None, :]
    weight = screened(squared) * (1.0 / (columns * rows * depth))
    weight = weight.reshape(share // 2, depth, 2 * columns)

    grid_shape = (blocks, piece, rows, columns)
    out = jnp.zeros((count, blocks, 2, piece // 2, rows, columns), jnp.float32)
    split = orbitals.reshape((count,) + grid_shape)
    moved = []
    for index in range(count):
        parts = []
        for step in range(blocks):
            part = lax.dynamic_slice(
                split, (index, band ^ step, 0, 0, 0), (1, 1, piece, rows, columns)
            ).reshape(piece, rows, columns)
            if step:
                if index:
                    part = after(part, moved[index - 1][1])
                part = lax.ppermute(part, "band", [(at, at ^ step) for at in range(blocks)])
            parts.append(part)
        moved.append(parts)
    tables = (out, across, along, along_back, forth, back, weight)
    moved[1][0], out, across, along, along_back, forth, back, weight = lax.optimization_barrier(
        (moved[1][0],) + tables
    )

    def gather(index, shift, *earlier):
        parts = []
        for step in range(blocks):
            block = ((layer ^ step) + (blocks - shift)) % blocks
            part = lax.select_n(block ^ band, *moved[index])
            if earlier:
                part = after(part, *earlier)
            if step:
                part = lax.ppermute(part, "layer", [(at, at ^ step) for at in range(blocks)])
            parts.append(part)
        return parts

    known = {}
    for index in range(count):
        known[index] = gather(index, 0, *(known[index - 1][1:] if index else ()))

    def exchange(values):
        axes = ("inner", "band")
        return [
            lax.ppermute(value, axes, [(at, at ^ place % group) for at in range(group)])
            if place % group
            else value
            for place, value in enumerate(values)
        ]

    batches = batch_list(count)
    held, state = {}, {}
    previous = []

    def begin(step):
        order = int(step[1:])
        right = after(across, *previous)
        values = forward(batches[order], known, group, along, right)
        previous[:] = values[:1]
        state[step[1:]] = exchange(values)

    def middle(step):
        weights = after(weight, *previous)
        parts = 2 if step[1:] + "b" in ends else 1
        values = through_depth(state[step[1:]], planes, parts, forth, back, weights)
        previous[:] = values[:1]
        values = exchange(values)
        state[step[1:]], state[step[1:] + "b"] = values[:group], values[group:]

    def finish(step):
        order = int(step[1:].rstrip("b"))
        begin = planes // 2 if step.endswith("b") else 0
        right = after(across, *previous)
        uses = [[(i, j)] + ([(j, i)] if i != j < count else []) for i, j in batches[order]]
        results = inverse(state[step[1:]], uses, known, held, begin, along_back, right)
        previous[:] = [results[uses[0][0][0]]]
        if step[1:] + "b" in ends or step.endswith("b"):
            halves_of.append(results[count - 1])
        else:
            held.update(results)

    for index in range(count):
        known[count + index] = gather(index, 1, *known[count - 1][1:])
    steps = schedule(count)
    ends = {step[1:] for step in steps if step.endswith("b")}
    halves_of = []
    for step in steps:
        {"f": begin, "d": middle, "i": finish}[step[0]](step)

    everywhere = ("layer", "inner", "band")

    def route(step):
        spot = lambda at, within, along: (at * inner + within) * blocks + along
        return [
            (spot(q, i, b), spot(b ^ step, i, q))
            for q in range(blocks)
            for i in range(inner)
            for b in range(blocks)
        ]

    results = [(index, 0, held[index]) for index in range(count - 1)]
    results += [(count - 1, half, value) for half, value in enumerate(halves_of)]
    for index, half, result in results:
        result = result.reshape(-1, blocks, piece // 2, rows, columns)
        for step in range(blocks):
            part = lax.dynamic_index_in_dim(result, layer ^ band ^ step, 1, keepdims=False)
            part = lax.ppermute(part, everywhere, route(step))
            spot = (index, layer ^ step, half, 0, 0, 0)
            out = lax.dynamic_update_slice(out, part[None, None], spot)
    return out.reshape(count, planes, rows, columns)


def exchange_sum(value, split_axis, concat_axis):
    return lax.all_to_all(value, "slab", split_axis=split_axis, concat_axis=concat_axis, tiled=True)


def plain_body(orbitals):
    count, planes, rows, columns = orbitals.shape
    depth = planes * lax.axis_size("slab")
    blocks = lax.axis_size("band")
    pairs = [(source, (source + 1) % blocks) for source in range(blocks)]
    neighbour = lax.ppermute(orbitals, "band", pairs)
    x_count = jnp.arange(columns, dtype=jnp.int32)
    y_count = jnp.arange(rows, dtype=jnp.int32)
    z_count = jnp.arange(depth, dtype=jnp.int32)
    cas_x = cas_table(x_count, x_count, columns)
    cas_y = cas_table(y_count, y_count, rows)
    cas_z = cas_table(z_count, z_count, depth)
    slabs = lax.axis_size("slab")
    split_axis, extent = (2, rows) if rows % slabs == 0 else (3, columns)
    share = extent // slabs
    mine = lax.axis_index("slab") * share + jnp.arange(share, dtype=jnp.int32)
    y_rows, x_rows = (mine, x_count) if split_axis == 2 else (y_count, mine)
    squared = ((2.0 * math.pi / depth * frequency(z_count, depth)) ** 2)[:, None, None]
    squared = squared + ((2.0 * math.pi / rows * frequency(y_rows, rows)) ** 2)[None, :, None]
    squared = squared + ((2.0 * math.pi / columns * frequency(x_rows, columns)) ** 2)[None, None, :]
    weight = screened(squared) * (1.0 / (columns * rows * depth))
    result = jnp.zeros_like(orbitals)
    for partners in (orbitals, neighbour):
        density = (orbitals[:, None] * partners[None, :]).reshape((-1, planes, rows, columns))
        value = jnp.einsum("pzyx,xk->pzyk", density, cas_x, precision=highest)
        value = jnp.einsum("pzyx,yk->pzkx", value, cas_y, precision=highest)
        value = exchange_sum(value, split_axis, 1)
        value = jnp.einsum("pzyx,zk->pkyx", value, cas_z, precision=highest) * weight
        value = jnp.einsum("pzyx,zk->pkyx", value, cas_z, precision=highest)
        value = exchange_sum(value, 1, split_axis)
        value = jnp.einsum("pzyx,yk->pzkx", value, cas_y, precision=highest)
        value = jnp.einsum("pzyx,xk->pzyk", value, cas_x, precision=highest)
        field = value.reshape((count, count, planes, rows, columns))
        result = result - jnp.sum(field * partners[None], axis=1)
    return result


def solution(mesh):
    slabs, blocks = mesh.shape["slab"], mesh.shape["band"]

    def run(orbitals):
        planes = orbitals.shape[1] // slabs
        rows, columns = orbitals.shape[2:]
        inner = max(slabs // blocks, 1)
        share = rows // (inner * blocks)
        fits = slabs % blocks == 0 and planes % (4 * blocks) == 0 and planes % 16 == 0
        fits = fits and slabs & (slabs - 1) == 0 and blocks & (blocks - 1) == 0
        fits = fits and rows % (inner * blocks) == 0 and share % 8 == 0 and columns % 128 == 0
        if not fits:
            spec = P("band", "slab", None, None)
            return jax.shard_map(
                plain_body, mesh=mesh, in_specs=(spec,), out_specs=spec, check_vma=False
            )(orbitals)
        finer = Mesh(mesh.devices.reshape(blocks, inner, blocks), ("layer", "inner", "band"))
        spec = P("band", ("layer", "inner"), None, None)
        step = jax.shard_map(
            layered_body, mesh=finer, in_specs=(spec,), out_specs=spec, check_vma=False
        )
        return step(orbitals)

    return run
```

profile of v0, /device:TPU:0, one launch (start us, length us, event | category | flops | bytes accessed | tf_op | source)
XLA Modules:
  0.0 378.4 jit_solution(11444105667269768391)
XLA Ops:
  0.0 2.7 dynamic-slice_bitcast_fusion.6
  12.1 5.8 %collective-permute-done.1 = f32[4,128,128]{2,1,0:T(8,128)} collective-permute-done((f32[4,128,128]{2,1,0:T(8,128)}, f32[4,128,128]{2,1,0:T(8,128)}, u32[]{:S(2)}, u32[]{:S(2)}) %collective-permute-start.1) | collective-permute-done | bytes 262176 | tf_op jit(solution)/shard_map/ppermute | solution.py:312
  19.9 4.4 %collective-permute-start.5 = (f32[4,128,128]{2,1,0:T(8,128)S(1)}, f32[4,128,128]{2,1,0:T(8,128)S(1)}, u32[]{:S(2)}, u32[]{:S(2)}) collective-permute-start(f32[4,128,128]{2,1,0:T(8,128)S(1)} %get-tuple-element.303), channel_id=1, source_target_pairs={{0,24},{8,16},{16,8},{24,0},{1,25},{9,17},{17,9},{25,1},{2,26},{10... | collective-permute-start | bytes 786440 | tf_op jit(solution)/shard_map/ppermute | solution.py:328
  27.0 4.7 %collective-permute-done.5.refs_3_.refs_11_ = f32[4,128,128]{2,1,0:T(8,128)S(1)} collective-permute-done((f32[4,128,128]{2,1,0:T(8,128)S(1)}, f32[4,128,128]{2,1,0:T(8,128)S(1)}, u32[]{:S(2)}, u32[]{:S(2)}) %collective-permute-start.5) | collective-permute-done | bytes 262176 | tf_op jit(solution)/shard_map/ppermute | solution.py:328
  33.4 13.5 %collective-permute-done.4.refs_2_.refs_10_ = f32[4,128,128]{2,1,0:T(8,128)S(1)} collective-permute-done((f32[4,128,128]{2,1,0:T(8,128)}, f32[4,128,128]{2,1,0:T(8,128)S(1)}, u32[]{:S(2)}, u32[]{:S(2)}) %collective-permute-start.4) | collective-permute-done | bytes 262176 | tf_op jit(solution)/shard_map/ppermute | solution.py:328
  51.7 2.5 collective-permute-start.11
  58.7 4.7 %collective-permute-done.10.refs_5_ = f32[1,256,128]{2,1,0:T(8,128)S(1)} collective-permute-done((f32[1,256,128]{2,1,0:T(8,128)S(1)}, f32[1,256,128]{2,1,0:T(8,128)S(1)}, u32[]{:S(2)}, u32[]{:S(2)}) %collective-permute-start.10) | collective-permute-done | bytes 131104 | tf_op jit(solution)/shard_map/ppermute | solution.py:339
  68.3 7.3 %collective-permute-done.16.refs_5_.refs_1_.refs_13_.refs_9_ = f32[4,128,128]{2,1,0:T(8,128)S(1)} collective-permute-done((f32[4,128,128]{2,1,0:T(8,128)S(1)}, f32[4,128,128]{2,1,0:T(8,128)S(1)}, u32[]{:S(2)}, u32[]{:S(2)}) %collective-permute-start.16) | collective-permute-done | bytes 262176 | tf_op jit(solution)/shard_map/ppermute | solution.py:328
  77.2 4.2 %collective-permute-done.17.refs_6_.refs_2_.refs_14_.refs_10_ = f32[4,128,128]{2,1,0:T(8,128)S(1)} collective-permute-done((f32[4,128,128]{2,1,0:T(8,128)S(1)}, f32[4,128,128]{2,1,0:T(8,128)S(1)}, u32[]{:S(2)}, u32[]{:S(2)}) %collective-permute-start.17) | collective-permute-done | bytes 262176 | tf_op jit(solution)/shard_map/ppermute | solution.py:328
  88.0 4.2 %collective-permute-done.23.refs_5_ = f32[1,256,128]{2,1,0:T(8,128)S(1)} collective-permute-done((f32[1,256,128]{2,1,0:T(8,128)S(1)}, f32[1,256,128]{2,1,0:T(8,128)S(1)}, u32[]{:S(2)}, u32[]{:S(2)}) %collective-permute-start.23) | collective-permute-done | bytes 131104 | tf_op jit(solution)/shard_map/ppermute | solution.py:339
  99.5 5.9 %collective-permute-done.29.refs_4_ = f32[1,256,128]{2,1,0:T(8,128)S(1)} collective-permute-done((f32[1,256,128]{2,1,0:T(8,128)S(1)}, f32[1,256,128]{2,1,0:T(8,128)S(1)}, u32[]{:S(2)}, u32[]{:S(2)}) %collective-permute-start.29) | collective-permute-done | bytes 131104 | tf_op jit(solution)/shard_map/ppermute | solution.py:339
  115.8 5.1 %collective-permute-done.37.refs_5_ = f32[1,256,128]{2,1,0:T(8,128)S(1)} collective-permute-done((f32[1,256,128]{2,1,0:T(8,128)S(1)}, f32[1,256,128]{2,1,0:T(8,128)S(1)}, u32[]{:S(2)}, u32[]{:S(2)}) %collective-permute-start.37) | collective-permute-done | bytes 131104 | tf_op jit(solution)/shard_map/ppermute | solution.py:339
  130.4 5.1 %collective-permute-done.47.refs_5_ = f32[1,256,128]{2,1,0:T(8,128)S(1)} collective-permute-done((f32[1,256,128]{2,1,0:T(8,128)S(1)}, f32[1,256,128]{2,1,0:T(8,128)S(1)}, u32[]{:S(2)}, u32[]{:S(2)}) %collective-permute-start.47) | collective-permute-done | bytes 131104 | tf_op jit(solution)/shard_map/ppermute | solution.py:339
  142.5 3.9 %collective-permute-done.56.refs_4_ = f32[1,256,128]{2,1,0:T(8,128)S(1)} collective-permute-done((f32[1,256,128]{2,1,0:T(8,128)S(1)}, f32[1,256,128]{2,1,0:T(8,128)S(1)}, u32[]{:S(2)}, u32[]{:S(2)}) %collective-permute-start.56) | collective-permute-done | bytes 131104 | tf_op jit(solution)/shard_map/ppermute | solution.py:339
  152.3 5.7 %collective-permute-done.41.refs_6_.refs_10_ = f32[4,128,128]{2,1,0:T(8,128)S(1)} collective-permute-done((f32[4,128,128]{2,1,0:T(8,128)S(1)}, f32[4,128,128]{2,1,0:T(8,128)S(1)}, u32[]{:S(2)}, u32[]{:S(2)}) %collective-permute-start.41) | collective-permute-done | bytes 262176 | tf_op jit(solution)/shard_map/ppermute | solution.py:328
  160.9 3.0 collective-permute-done.58.refs_6_
  164.0 2.7 collective-permute-done.59.refs_7_
  168.1 12.4 %collective-permute-done.51.refs_6_.refs_10_.refs_14_ = f32[4,128,128]{2,1,0:T(8,128)S(1)} collective-permute-done((f32[4,128,128]{2,1,0:T(8,128)S(1)}, f32[4,128,128]{2,1,0:T(8,128)S(1)}, u32[]{:S(2)}, u32[]{:S(2)}) %collective-permute-start.51) | collective-permute-done | bytes 262176 | tf_op jit(solution)/shard_map/ppermute | solution.py:328
  188.3 5.1 %collective-permute-done.64.refs_5_ = f32[1,256,128]{2,1,0:T(8,128)S(1)} collective-permute-done((f32[1,256,128]{2,1,0:T(8,128)S(1)}, f32[1,256,128]{2,1,0:T(8,128)S(1)}, u32[]{:S(2)}, u32[]{:S(2)}) %collective-permute-start.64) | collective-permute-done | bytes 131104 | tf_op jit(solution)/shard_map/ppermute | solution.py:339
  203.0 5.2 %collective-permute-done.71.refs_5_ = f32[1,256,128]{2,1,0:T(8,128)S(1)} collective-permute-done((f32[1,256,128]{2,1,0:T(8,128)S(1)}, f32[1,256,128]{2,1,0:T(8,128)S(1)}, u32[]{:S(2)}, u32[]{:S(2)}) %collective-permute-start.71) | collective-permute-done | bytes 131104 | tf_op jit(solution)/shard_map/ppermute | solution.py:339
  221.8 4.1 %collective-permute-done.80.refs_7_ = f32[1,256,128]{2,1,0:T(8,128)S(1)} collective-permute-done((f32[1,256,128]{2,1,0:T(8,128)S(1)}, f32[1,256,128]{2,1,0:T(8,128)S(1)}, u32[]{:S(2)}, u32[]{:S(2)}) %collective-permute-start.80) | collective-permute-done | bytes 131104 | tf_op jit(solution)/shard_map/ppermute | solution.py:339
  236.2 12.8 %collective-permute-done.84.refs_4_ = f32[2,256,128]{2,1,0:T(8,128)S(1)} collective-permute-done((f32[2,256,128]{2,1,0:T(8,128)S(1)}, f32[2,256,128]{2,1,0:T(8,128)S(1)}, u32[]{:S(2)}, u32[]{:S(2)}) %collective-permute-start.84) | collective-permute-done | bytes 262176 | tf_op jit(solution)/shard_map/ppermute | solution.py:339
  249.9 3.1 collective-permute-done.85.refs_5_
  289.8 5.4 %collective-permute-done.103.refs_5_ = f32[2,128,128]{2,1,0:T(8,128)S(1)} collective-permute-done((f32[2,128,128]{2,1,0:T(8,128)S(1)}, f32[2,128,128]{2,1,0:T(8,128)S(1)}, u32[]{:S(2)}, u32[]{:S(2)}) %collective-permute-start.103) | collective-permute-done | bytes 131104 | tf_op jit(solution)/shard_map/ppermute | solution.py:339
  303.7 5.0 %collective-permute-done.113.refs_4_ = f32[2,128,128]{2,1,0:T(8,128)S(1)} collective-permute-done((f32[2,128,128]{2,1,0:T(8,128)S(1)}, f32[2,128,128]{2,1,0:T(8,128)S(1)}, u32[]{:S(2)}, u32[]{:S(2)}) %collective-permute-start.113) | collective-permute-done | bytes 131104 | tf_op jit(solution)/shard_map/ppermute | solution.py:339
  308.7 3.7 collective-permute-start.97
  314.1 6.4 %collective-permute-start.120 = (f32[1,2,128,128]{3,2,1,0:T(8,128)S(1)}, f32[1,2,128,128]{3,2,1,0:T(8,128)S(1)}, u32[]{:S(2)}, u32[]{:S(2)}) collective-permute-start(f32[1,2,128,128]{3,2,1,0:T(8,128)S(1)} %get-tuple-element.326), channel_id=1, source_target_pairs={{0,24},{1,16},{2,8},{3,0},{4,28},{5,20},{6,12},{7,4},{8,25},{9,17}... | collective-permute-start | bytes 393224 | tf_op jit(solution)/shard_map/ppermute | solution.py:401
  320.5 16.4 %collective-permute-start.119 = (f32[1,2,128,128]{3,2,1,0:T(8,128)S(1)}, f32[1,2,128,128]{3,2,1,0:T(8,128)S(1)}, u32[]{:S(2)}, u32[]{:S(2)}) collective-permute-start(f32[1,2,128,128]{3,2,1,0:T(8,128)S(1)} %get-tuple-element.327), channel_id=1, source_target_pairs={{0,16},{1,24},{2,0},{3,8},{4,20},{5,28},{6,4},{7,12},{8,17},{9,25}... | collective-permute-start | bytes 393224 | tf_op jit(solution)/shard_map/ppermute | solution.py:401
  339.8 8.4 %collective-permute-start.107 = (f32[1,2,128,128]{3,2,1,0:T(8,128)S(1)}, f32[1,2,128,128]{3,2,1,0:T(8,128)S(1)}, u32[]{:S(2)}, u32[]{:S(2)}) collective-permute-start(f32[1,2,128,128]{3,2,1,0:T(8,128)S(1)} %get-tuple-element.332), channel_id=1, source_target_pairs={{0,8},{1,0},{2,24},{3,16},{4,12},{5,4},{6,28},{7,20},{8,9},{9,1},{... | collective-permute-start | bytes 393224 | tf_op jit(solution)/shard_map/ppermute | solution.py:401
  350.8 14.1 %collective-permute-start.108 = (f32[1,2,128,128]{3,2,1,0:T(8,128)S(1)}, f32[1,2,128,128]{3,2,1,0:T(8,128)S(1)}, u32[]{:S(2)}, u32[]{:S(2)}) collective-permute-start(f32[1,2,128,128]{3,2,1,0:T(8,128)S(1)} %get-tuple-element.331), channel_id=1, source_target_pairs={{0,16},{1,24},{2,0},{3,8},{4,20},{5,28},{6,4},{7,12},{8,17},{9,25}... | collective-permute-start | bytes 393224 | tf_op jit(solution)/shard_map/ppermute | solution.py:401
  364.9 6.3 %collective-permute-done.108 = f32[1,2,128,128]{3,2,1,0:T(8,128)S(1)} collective-permute-done((f32[1,2,128,128]{3,2,1,0:T(8,128)S(1)}, f32[1,2,128,128]{3,2,1,0:T(8,128)S(1)}, u32[]{:S(2)}, u32[]{:S(2)}) %collective-permute-start.108) | collective-permute-done | bytes 131104 | tf_op jit(solution)/shard_map/ppermute | solution.py:401
  372.7 4.2 %collective-permute-done.109 = f32[1,2,128,128]{3,2,1,0:T(8,128)S(1)} collective-permute-done((f32[1,2,128,128]{3,2,1,0:T(8,128)S(1)}, f32[1,2,128,128]{3,2,1,0:T(8,128)S(1)}, u32[]{:S(2)}, u32[]{:S(2)}) %collective-permute-start.109) | collective-permute-done | bytes 131104 | tf_op jit(solution)/shard_map/ppermute | solution.py:401
  (396 shorter events, 179.1 us)
Async XLA Ops:
  24.4 22.5 %collective-permute-start.4 = (f32[4,128,128]{2,1,0:T(8,128)}, f32[4,128,128]{2,1,0:T(8,128)S(1)}, u32[]{:S(2)}, u32[]{:S(2)}) collective-permute-start(f32[4,128,128]{2,1,0:T(8,128)} %get-tuple-element.304), channel_id=1, source_target_pairs={{0,16},{8,24},{16,0},{24,8},{1,17},{9,25},{17,1},{25,9},{2,18},{10... | collective-permute-start | bytes 786440 | tf_op jit(solution)/shard_map/ppermute | solution.py:328
  24.5 22.4 %collective-permute-start.3 = (f32[4,128,128]{2,1,0:T(8,128)}, f32[4,128,128]{2,1,0:T(8,128)S(1)}, u32[]{:S(2)}, u32[]{:S(2)}) collective-permute-start(f32[4,128,128]{2,1,0:T(8,128)} %get-tuple-element.305), channel_id=1, source_target_pairs={{0,8},{8,0},{16,24},{24,16},{1,9},{9,1},{17,25},{25,17},{2,10},{10... | collective-permute-start | bytes 786440 | tf_op jit(solution)/shard_map/ppermute | solution.py:328
  25.2 24.3 %collective-permute-start.14 = (f32[4,128,128]{2,1,0:T(8,128)}, f32[4,128,128]{2,1,0:T(8,128)S(1)}, u32[]{:S(2)}, u32[]{:S(2)}) collective-permute-start(f32[4,128,128]{2,1,0:T(8,128)} %get-tuple-element.172), channel_id=1, source_target_pairs={{0,2},{1,3},{2,0},{3,1},{4,6},{5,7},{6,4},{7,5},{8,10},{9,11},{10,... | collective-permute-start | bytes 786440 | tf_op jit(solution)/shard_map/ppermute | solution.py:312
  27.0 22.8 %collective-permute-start.15 = (f32[4,128,128]{2,1,0:T(8,128)}, f32[4,128,128]{2,1,0:T(8,128)S(1)}, u32[]{:S(2)}, u32[]{:S(2)}) collective-permute-start(f32[4,128,128]{2,1,0:T(8,128)} %get-tuple-element.173), channel_id=1, source_target_pairs={{0,3},{1,2},{2,1},{3,0},{4,7},{5,6},{6,5},{7,4},{8,11},{9,10},{10,... | collective-permute-start | bytes 786440 | tf_op jit(solution)/shard_map/ppermute | solution.py:312
  31.7 19.7 %collective-permute-start.13 = (f32[4,128,128]{2,1,0:T(8,128)S(1)}, f32[4,128,128]{2,1,0:T(8,128)S(1)}, u32[]{:S(2)}, u32[]{:S(2)}) collective-permute-start(f32[4,128,128]{2,1,0:T(8,128)S(1)} %copy-done.60), channel_id=1, source_target_pairs={{0,1},{1,0},{2,3},{3,2},{4,5},{5,4},{6,7},{7,6},{8,9},{9,8},{10,11... | collective-permute-start | bytes 786440 | tf_op jit(solution)/shard_map/ppermute | solution.py:312
  63.4 18.0 %collective-permute-start.17 = (f32[4,128,128]{2,1,0:T(8,128)S(1)}, f32[4,128,128]{2,1,0:T(8,128)S(1)}, u32[]{:S(2)}, u32[]{:S(2)}) collective-permute-start(f32[4,128,128]{2,1,0:T(8,128)S(1)} %get-tuple-element.176), channel_id=1, source_target_pairs={{0,16},{8,24},{16,0},{24,8},{1,17},{9,25},{17,1},{25,9},{2,18},{10... | collective-permute-start | bytes 786440 | tf_op jit(solution)/shard_map/ppermute | solution.py:328
  64.3 18.3 %collective-permute-start.19 = (f32[1,256,128]{2,1,0:T(8,128)S(1)}, f32[1,256,128]{2,1,0:T(8,128)S(1)}, u32[]{:S(2)}, u32[]{:S(2)}) collective-permute-start(f32[1,256,128]{2,1,0:T(8,128)S(1)} %get-tuple-element.182), channel_id=1, source_target_pairs={{0,1},{1,0},{2,3},{3,2},{4,5},{5,4},{6,7},{7,6},{8,9},{9,8},{10,11... | collective-permute-start | bytes 393224 | tf_op jit(solution)/shard_map/ppermute | solution.py:339
  65.1 19.7 %collective-permute-start.20 = (f32[1,256,128]{2,1,0:T(8,128)S(1)}, f32[1,256,128]{2,1,0:T(8,128)S(1)}, u32[]{:S(2)}, u32[]{:S(2)}) collective-permute-start(f32[1,256,128]{2,1,0:T(8,128)S(1)} %get-tuple-element.183), channel_id=1, source_target_pairs={{0,2},{1,3},{2,0},{3,1},{4,6},{5,7},{6,4},{7,5},{8,10},{9,11},{10,... | collective-permute-start | bytes 393224 | tf_op jit(solution)/shard_map/ppermute | solution.py:339
  67.3 19.0 %collective-permute-start.21 = (f32[1,256,128]{2,1,0:T(8,128)S(1)}, f32[1,256,128]{2,1,0:T(8,128)S(1)}, u32[]{:S(2)}, u32[]{:S(2)}) collective-permute-start(f32[1,256,128]{2,1,0:T(8,128)S(1)} %get-tuple-element.184), channel_id=1, source_target_pairs={{0,3},{1,2},{2,1},{3,0},{4,7},{5,6},{6,5},{7,4},{8,11},{9,10},{10,... | collective-permute-start | bytes 393224 | tf_op jit(solution)/shard_map/ppermute | solution.py:339
  136.6 21.5 %collective-permute-start.41 = (f32[4,128,128]{2,1,0:T(8,128)S(1)}, f32[4,128,128]{2,1,0:T(8,128)S(1)}, u32[]{:S(2)}, u32[]{:S(2)}) collective-permute-start(f32[4,128,128]{2,1,0:T(8,128)S(1)} %get-tuple-element.210), channel_id=1, source_target_pairs={{0,16},{8,24},{16,0},{24,8},{1,17},{9,25},{17,1},{25,9},{2,18},{10... | collective-permute-start | bytes 786440 | tf_op jit(solution)/shard_map/ppermute | solution.py:328
  138.5 21.5 %collective-permute-start.42 = (f32[4,128,128]{2,1,0:T(8,128)S(1)}, f32[4,128,128]{2,1,0:T(8,128)S(1)}, u32[]{:S(2)}, u32[]{:S(2)}) collective-permute-start(f32[4,128,128]{2,1,0:T(8,128)S(1)} %get-tuple-element.211), channel_id=1, source_target_pairs={{0,24},{8,16},{16,8},{24,0},{1,25},{9,17},{17,9},{25,1},{2,26},{10... | collective-permute-start | bytes 786440 | tf_op jit(solution)/shard_map/ppermute | solution.py:328
  146.4 21.3 %collective-permute-start.50 = (f32[4,128,128]{2,1,0:T(8,128)S(1)}, f32[4,128,128]{2,1,0:T(8,128)S(1)}, u32[]{:S(2)}, u32[]{:S(2)}) collective-permute-start(f32[4,128,128]{2,1,0:T(8,128)S(1)} %get-tuple-element.224), channel_id=1, source_target_pairs={{0,8},{8,0},{16,24},{24,16},{1,9},{9,1},{17,25},{25,17},{2,10},{10... | collective-permute-start | bytes 786440 | tf_op jit(solution)/shard_map/ppermute | solution.py:328
  148.2 32.2 %collective-permute-start.51 = (f32[4,128,128]{2,1,0:T(8,128)S(1)}, f32[4,128,128]{2,1,0:T(8,128)S(1)}, u32[]{:S(2)}, u32[]{:S(2)}) collective-permute-start(f32[4,128,128]{2,1,0:T(8,128)S(1)} %get-tuple-element.225), channel_id=1, source_target_pairs={{0,16},{8,24},{16,0},{24,8},{1,17},{9,25},{17,1},{25,9},{2,18},{10... | collective-permute-start | bytes 786440 | tf_op jit(solution)/shard_map/ppermute | solution.py:328
  150.6 31.3 %collective-permute-start.52 = (f32[4,128,128]{2,1,0:T(8,128)S(1)}, f32[4,128,128]{2,1,0:T(8,128)S(1)}, u32[]{:S(2)}, u32[]{:S(2)}) collective-permute-start(f32[4,128,128]{2,1,0:T(8,128)S(1)} %get-tuple-element.226), channel_id=1, source_target_pairs={{0,24},{8,16},{16,8},{24,0},{1,25},{9,17},{17,9},{25,1},{2,26},{10... | collective-permute-start | bytes 786440 | tf_op jit(solution)/shard_map/ppermute | solution.py:328
  164.0 19.0 %collective-permute-start.60 = (f32[1,256,128]{2,1,0:T(8,128)S(1)}, f32[1,256,128]{2,1,0:T(8,128)S(1)}, u32[]{:S(2)}, u32[]{:S(2)}) collective-permute-start(f32[1,256,128]{2,1,0:T(8,128)S(1)} %get-tuple-element.238), channel_id=1, source_target_pairs={{0,1},{1,0},{2,3},{3,2},{4,5},{5,4},{6,7},{7,6},{8,9},{9,8},{10,11... | collective-permute-start | bytes 393224 | tf_op jit(solution)/shard_map/ppermute | solution.py:339
  167.7 19.2 %collective-permute-start.62 = (f32[1,256,128]{2,1,0:T(8,128)S(1)}, f32[1,256,128]{2,1,0:T(8,128)S(1)}, u32[]{:S(2)}, u32[]{:S(2)}) collective-permute-start(f32[1,256,128]{2,1,0:T(8,128)S(1)} %get-tuple-element.240), channel_id=1, source_target_pairs={{0,3},{1,2},{2,1},{3,0},{4,7},{5,6},{6,5},{7,4},{8,11},{9,10},{10,... | collective-permute-start | bytes 393224 | tf_op jit(solution)/shard_map/ppermute | solution.py:339
  228.6 20.4 %collective-permute-start.84 = (f32[2,256,128]{2,1,0:T(8,128)S(1)}, f32[2,256,128]{2,1,0:T(8,128)S(1)}, u32[]{:S(2)}, u32[]{:S(2)}) collective-permute-start(f32[2,256,128]{2,1,0:T(8,128)S(1)} %get-tuple-element.269), channel_id=1, source_target_pairs={{0,4},{1,5},{2,6},{3,7},{4,0},{5,1},{6,2},{7,3},{8,12},{9,13},{10,... | collective-permute-start | bytes 786440 | tf_op jit(solution)/shard_map/ppermute | solution.py:339
  230.1 22.9 %collective-permute-start.85 = (f32[2,256,128]{2,1,0:T(8,128)S(1)}, f32[2,256,128]{2,1,0:T(8,128)S(1)}, u32[]{:S(2)}, u32[]{:S(2)}) collective-permute-start(f32[2,256,128]{2,1,0:T(8,128)S(1)} %get-tuple-element.270), channel_id=1, source_target_pairs={{0,5},{1,4},{2,7},{3,6},{4,1},{5,0},{6,3},{7,2},{8,13},{9,12},{10,... | collective-permute-start | bytes 786440 | tf_op jit(solution)/shard_map/ppermute | solution.py:339
  230.3 24.7 %collective-permute-start.86 = (f32[2,256,128]{2,1,0:T(8,128)S(1)}, f32[2,256,128]{2,1,0:T(8,128)S(1)}, u32[]{:S(2)}, u32[]{:S(2)}) collective-permute-start(f32[2,256,128]{2,1,0:T(8,128)S(1)} %get-tuple-element.271), channel_id=1, source_target_pairs={{0,6},{1,7},{2,4},{3,5},{4,2},{5,3},{6,0},{7,1},{8,14},{9,15},{10,... | collective-permute-start | bytes 786440 | tf_op jit(solution)/shard_map/ppermute | solution.py:339
  231.8 24.6 %collective-permute-start.87 = (f32[2,256,128]{2,1,0:T(8,128)S(1)}, f32[2,256,128]{2,1,0:T(8,128)S(1)}, u32[]{:S(2)}, u32[]{:S(2)}) collective-permute-start(f32[2,256,128]{2,1,0:T(8,128)S(1)} %get-tuple-element.272), channel_id=1, source_target_pairs={{0,7},{1,6},{2,5},{3,4},{4,3},{5,2},{6,1},{7,0},{8,15},{9,14},{10,... | collective-permute-start | bytes 786440 | tf_op jit(solution)/shard_map/ppermute | solution.py:339
  234.6 32.5 %collective-permute-start.90 = (f32[1,256,128]{2,1,0:T(8,128)S(1)}, f32[1,256,128]{2,1,0:T(8,128)S(1)}, u32[]{:S(2)}, u32[]{:S(2)}) collective-permute-start(f32[1,256,128]{2,1,0:T(8,128)S(1)} %get-tuple-element.277), channel_id=1, source_target_pairs={{0,3},{1,2},{2,1},{3,0},{4,7},{5,6},{6,5},{7,4},{8,11},{9,10},{10,... | collective-permute-start | bytes 393224 | tf_op jit(solution)/shard_map/ppermute | solution.py:339
  249.0 20.0 %collective-permute-start.91 = (f32[1,256,128]{2,1,0:T(8,128)S(1)}, f32[1,256,128]{2,1,0:T(8,128)S(1)}, u32[]{:S(2)}, u32[]{:S(2)}) collective-permute-start(f32[1,256,128]{2,1,0:T(8,128)S(1)} %get-tuple-element.278), channel_id=1, source_target_pairs={{0,4},{1,5},{2,6},{3,7},{4,0},{5,1},{6,2},{7,3},{8,12},{9,13},{10,... | collective-permute-start | bytes 393224 | tf_op jit(solution)/shard_map/ppermute | solution.py:339
  267.8 18.0 %collective-permute-start.99 = (f32[2,128,128]{2,1,0:T(8,128)}, f32[2,128,128]{2,1,0:T(8,128)S(1)}, u32[]{:S(2)}, u32[]{:S(2)}) collective-permute-start(f32[2,128,128]{2,1,0:T(8,128)} %get-tuple-element.283), channel_id=1, source_target_pairs={{0,1},{1,0},{2,3},{3,2},{4,5},{5,4},{6,7},{7,6},{8,9},{9,8},{10,11... | collective-permute-start | bytes 393224 | tf_op jit(solution)/shard_map/ppermute | solution.py:339
  269.7 17.6 %collective-permute-start.100 = (f32[2,128,128]{2,1,0:T(8,128)}, f32[2,128,128]{2,1,0:T(8,128)S(1)}, u32[]{:S(2)}, u32[]{:S(2)}) collective-permute-start(f32[2,128,128]{2,1,0:T(8,128)} %get-tuple-element.284), channel_id=1, source_target_pairs={{0,2},{1,3},{2,0},{3,1},{4,6},{5,7},{6,4},{7,5},{8,10},{9,11},{10,... | collective-permute-start | bytes 393224 | tf_op jit(solution)/shard_map/ppermute | solution.py:339
  302.2 36.8 %collective-permute-start.98 = (f32[2,2,128,128]{3,2,1,0:T(8,128)S(1)}, f32[2,2,128,128]{3,2,1,0:T(8,128)S(1)}, u32[]{:S(2)}, u32[]{:S(2)}) collective-permute-start(f32[2,2,128,128]{3,2,1,0:T(8,128)S(1)} %get-tuple-element.314), channel_id=1, source_target_pairs={{0,24},{1,16},{2,8},{3,0},{4,28},{5,20},{6,12},{7,4},{8,25},{9,17}... | collective-permute-start | bytes 786440 | tf_op jit(solution)/shard_map/ppermute | solution.py:401
  308.7 29.6 %collective-permute-start.97 = (f32[2,2,128,128]{3,2,1,0:T(8,128)S(1)}, f32[2,2,128,128]{3,2,1,0:T(8,128)S(1)}, u32[]{:S(2)}, u32[]{:S(2)}) collective-permute-start(f32[2,2,128,128]{3,2,1,0:T(8,128)S(1)} %get-tuple-element.315), channel_id=1, source_target_pairs={{0,16},{1,24},{2,0},{3,8},{4,20},{5,28},{6,4},{7,12},{8,17},{9,25}... | collective-permute-start | bytes 786440 | tf_op jit(solution)/shard_map/ppermute | solution.py:401
  312.4 24.8 %collective-permute-start.96 = (f32[2,2,128,128]{3,2,1,0:T(8,128)S(1)}, f32[2,2,128,128]{3,2,1,0:T(8,128)S(1)}, u32[]{:S(2)}, u32[]{:S(2)}) collective-permute-start(f32[2,2,128,128]{3,2,1,0:T(8,128)S(1)} %get-tuple-element.316), channel_id=1, source_target_pairs={{0,8},{1,0},{2,24},{3,16},{4,12},{5,4},{6,28},{7,20},{8,9},{9,1},{... | collective-permute-start | bytes 786440 | tf_op jit(solution)/shard_map/ppermute | solution.py:401
  314.1 63.0 %collective-permute-start.120 = (f32[1,2,128,128]{3,2,1,0:T(8,128)S(1)}, f32[1,2,128,128]{3,2,1,0:T(8,128)S(1)}, u32[]{:S(2)}, u32[]{:S(2)}) collective-permute-start(f32[1,2,128,128]{3,2,1,0:T(8,128)S(1)} %get-tuple-element.326), channel_id=1, source_target_pairs={{0,24},{1,16},{2,8},{3,0},{4,28},{5,20},{6,12},{7,4},{8,25},{9,17}... | collective-permute-start | bytes 393224 | tf_op jit(solution)/shard_map/ppermute | solution.py:401
  320.5 56.5 %collective-permute-start.119 = (f32[1,2,128,128]{3,2,1,0:T(8,128)S(1)}, f32[1,2,128,128]{3,2,1,0:T(8,128)S(1)}, u32[]{:S(2)}, u32[]{:S(2)}) collective-permute-start(f32[1,2,128,128]{3,2,1,0:T(8,128)S(1)} %get-tuple-element.327), channel_id=1, source_target_pairs={{0,16},{1,24},{2,0},{3,8},{4,20},{5,28},{6,4},{7,12},{8,17},{9,25}... | collective-permute-start | bytes 393224 | tf_op jit(solution)/shard_map/ppermute | solution.py:401
  337.2 39.8 %collective-permute-start.118 = (f32[1,2,128,128]{3,2,1,0:T(8,128)S(1)}, f32[1,2,128,128]{3,2,1,0:T(8,128)S(1)}, u32[]{:S(2)}, u32[]{:S(2)}) collective-permute-start(f32[1,2,128,128]{3,2,1,0:T(8,128)S(1)} %get-tuple-element.328), channel_id=1, source_target_pairs={{0,8},{1,0},{2,24},{3,16},{4,12},{5,4},{6,28},{7,20},{8,9},{9,1},{... | collective-permute-start | bytes 393224 | tf_op jit(solution)/shard_map/ppermute | solution.py:401
  338.4 38.6 %collective-permute-start.117 = (f32[1,2,128,128]{3,2,1,0:T(8,128)S(1)}, f32[1,2,128,128]{3,2,1,0:T(8,128)S(1)}, u32[]{:S(2)}, u32[]{:S(2)}) collective-permute-start(f32[1,2,128,128]{3,2,1,0:T(8,128)S(1)} %get-tuple-element.329), channel_id=1, source_target_pairs={{0,0},{1,8},{2,16},{3,24},{4,4},{5,12},{6,20},{7,28},{8,1},{9,9},{... | collective-permute-start | bytes 393224 | tf_op jit(solution)/shard_map/ppermute | solution.py:401
  350.8 20.3 %collective-permute-start.108 = (f32[1,2,128,128]{3,2,1,0:T(8,128)S(1)}, f32[1,2,128,128]{3,2,1,0:T(8,128)S(1)}, u32[]{:S(2)}, u32[]{:S(2)}) collective-permute-start(f32[1,2,128,128]{3,2,1,0:T(8,128)S(1)} %get-tuple-element.331), channel_id=1, source_target_pairs={{0,16},{1,24},{2,0},{3,8},{4,20},{5,28},{6,4},{7,12},{8,17},{9,25}... | collective-permute-start | bytes 393224 | tf_op jit(solution)/shard_map/ppermute | solution.py:401
  (154 other events, 2157.3 us)
where the time goes:
time: 380 us; the launch traced here: 378 us
  starting transfers between devices  167 us (44%)
  waiting for transfers between devices  153 us (40%)
  local copies, waits for them, and re-layouts  28 us (7%)
  Pallas kernels  21.3 us (6%)
  other arithmetic  8.57 us (2%)
    ppermute x91, starting transfers between devices, exchange(): lax.ppermute(value, axes, [(at, at ^ place % group) for at in range(group)])  93 us
    ppermute x91, waiting for transfers between devices, exchange(): lax.ppermute(value, axes, [(at, at ^ place % group) for at in range(group)])  82.4 us
    ppermute x12, starting transfers between devices, layered_body(): part = lax.ppermute(part, everywhere, route(step))  55.2 us
    ppermute x12, waiting for transfers between devices, gather(): lax.ppermute(part, 'layer', [(at, at ^ step) for at in range(blocks)])  50.9 us
    unnamed x130, local copies, waits for them, and re-layouts  22.5 us
    ppermute x12, starting transfers between devices, gather(): lax.ppermute(part, 'layer', [(at, at ^ step) for at in range(blocks)])  13.6 us
    ppermute x12, waiting for transfers between devices, layered_body(): part = lax.ppermute(part, everywhere, route(step))  13 us
    pallas_call x6, Pallas kernels, through_depth(): pl.pallas_call(functools.partial(depth_kernel, planes, group), grid=(coun...  7.62 us
  transfers between devices with their start and end apart: 121, of which 35 were waited for; matrix products, arithmetic and copies ran while one was open for 2% of the time, Pallas kernels for 6%

commit v1 on v0

--- a/solution.py
+++ b/solution.py
@@ -74,21 +74,21 @@
     return plane % half // reach, plane // half * reach + plane % reach
 
 
-def pair_at(refs, plane, planes, pieces):
+def pair_at(refs, lead, plane, planes, pieces):
     piece, place = spot_of(plane, planes, pieces)
-    return refs[piece][place : place + 2]
-
-
-def forward_kernel(group, pieces, pairs, left_ref, right_ref, *refs):
+    return refs[piece][lead, place : place + 2]
+
+
+def forward_kernel(group, pieces, leads, pairs, left_ref, right_ref, *refs):
     refs, out_refs = refs[:-group], refs[-group:]
-    piece, rows, columns = refs[0].shape
+    _, piece, rows, columns = refs[0].shape
     share = rows // group
     planes = piece * pieces
     orbitals = [refs[at : at + pieces] for at in range(0, len(refs), pieces)]
     for which, (first, second) in enumerate(pairs):
         for plane in range(0, planes, 2):
-            density = pair_at(orbitals[first], plane, planes, pieces)
-            density = density * pair_at(orbitals[second], plane, planes, pieces)
+            density = pair_at(orbitals[first], leads[first], plane, planes, pieces)
+            density = density * pair_at(orbitals[second], leads[second], plane, planes, pieces)
             part = times_right(density.reshape(2 * rows, columns), right_ref[...])
             part = times_left(left_ref[...], jnp.concatenate([part[:rows], part[rows:]], axis=1))
             for offset in range(2):
@@ -145,12 +145,12 @@
 
 
 def inverse_kernel(uses, names, pieces, group, begin, left_ref, right_ref, *refs):
-    factors, held, targets = names
+    factors, leads, held, targets = names
     in_refs, refs = refs[:group], refs[group:]
     factor_refs = {
         factor: refs[place * pieces : (place + 1) * pieces] for place, factor in enumerate(factors)
     }
-    planes = refs[0].shape[0] * pieces
+    planes = refs[0].shape[1] * pieces
     refs = refs[len(factors) * pieces :]
     held_refs, out_refs = dict(zip(held, refs)), dict(zip(targets, refs[len(held) :]))
     count = refs[-1].shape[0]
@@ -159,7 +159,8 @@
         for which, pairs in enumerate(uses):
             field = potential_planes(plane, count, which, left_ref, right_ref, in_refs)
             for target, factor in pairs:
-                term = field * pair_at(factor_refs[factor], begin + plane, planes, pieces)
+                spot = (leads[factor], begin + plane, planes, pieces)
+                term = field * pair_at(factor_refs[factor], *spot)
                 total[target] = total[target] - term if target in total else -term
         for target in targets:
             out_refs[target][plane : plane + 2] = total[target]
@@ -178,17 +179,18 @@
 
 def forward(pairs, known, group, left, right):
     used = sorted({index for pair in pairs for index in pair})
-    pieces = len(known[used[0]])
-    piece, rows, columns = known[used[0]][0].shape
+    pieces = len(known[used[0]][0])
+    _, piece, rows, columns = known[used[0]][0][0].shape
+    leads = [known[index][1] for index in used]
     chunk = jax.ShapeDtypeStruct((len(pairs), rows // group * piece * pieces, columns), jnp.float32)
     places = [(used.index(first), used.index(second)) for first, second in pairs]
     return pl.pallas_call(
-        functools.partial(forward_kernel, group, pieces, places),
+        functools.partial(forward_kernel, group, pieces, leads, places),
         out_shape=[chunk] * group,
         cost_estimate=cost(len(pairs)),
         compiler_params=grant,
         name="forward",
-    )(left, right, *[part for index in used for part in known[index]])
+    )(left, right, *[part for index in used for part in known[index][0]])
 
 
 def through_depth(values, planes, parts, forth, back, weight):
@@ -215,11 +217,12 @@
     factors = sorted({factor for pairs in uses for _, factor in pairs})
     targets = sorted({target for pairs in uses for target, _ in pairs})
     given = [target for target in targets if target in held]
-    pieces = len(known[factors[0]])
-    _, rows, columns = known[factors[0]][0].shape
+    pieces = len(known[factors[0]][0])
+    rows, columns = known[factors[0]][0][0].shape[2:]
+    leads = {factor: known[factor][1] for factor in factors}
     planes = values[0].shape[1] * len(values) // rows
     result = jax.ShapeDtypeStruct((planes, rows, columns), jnp.float32)
-    names = (factors, given, targets)
+    names = (factors, leads, given, targets)
     results = pl.pallas_call(
         functools.partial(inverse_kernel, uses, names, pieces, len(values), begin),
         out_shape=[result] * len(targets),
@@ -230,28 +233,29 @@
         left,
         right,
         *values,
-        *[part for factor in factors for part in known[factor]],
+        *[part for factor in factors for part in known[factor][0]],
         *[held[target] for target in given],
     )
     return dict(zip(targets, results))
 
 
 def batch_list(count):
-    batches = [[(i, j)] for j in range(count) for i in range(j + 1)]
-    batches += [[(i, count + j)] for i in range(count - 1) for j in range(count)]
-    return batches + [[(count - 1, count + j) for j in range(count)]]
+    own = [[(i, j)] for j in range(count) for i in range(j + 1)]
+    return own + [[(i, count + j)] for i in range(count) for j in range(count)]
 
 
 def schedule(count):
-    total = len(batch_list(count))
-    own, last = count * (count + 1) // 2, total - 1
+    own, total = count * (count + 1) // 2, count * (count + 1) // 2 + count * count
     order = ["f0", "d0"] + [f"f{batch}" for batch in range(1, own)] + ["i0"]
     order += [f"d{batch}" for batch in range(1, own)]
-    for batch in range(own, last):
-        order += [f"f{batch}"] + ([f"i{batch - own + 1}"] if batch - own + 1 < own else [])
-    order += [f"i{batch}" for batch in range(last - own + 1, own)]
-    order += [f"d{own}", f"f{last}"] + [f"d{batch}" for batch in range(own + 1, last)]
-    order += [f"i{batch}" for batch in range(own, last - 1)]
+    waiting = [f"i{batch}" for batch in range(1, own)]
+    for batch in range(own, own + 2):
+        order += [f"f{batch}"] + waiting[:1]
+        waiting = waiting[1:]
+    order += waiting + [f"d{own}"]
+    for batch in range(own + 2, total):
+        order += [f"f{batch}", f"d{batch - 1}", f"i{batch - 2}"]
+    last = total - 1
     return order + [f"d{last}", f"i{last - 1}", f"i{last}", f"i{last}b"]
 
 
@@ -302,9 +306,10 @@
     moved = []
     for index in range(count):
         parts = []
+        source = after(split, across) if index else split
         for step in range(blocks):
             part = lax.dynamic_slice(
-                split, (index, band ^ step, 0, 0, 0), (1, 1, piece, rows, columns)
+                source, (index, band ^ step, 0, 0, 0), (1, 1, piece, rows, columns)
             ).reshape(piece, rows, columns)
             if step:
                 if index:
@@ -317,11 +322,11 @@
         (moved[1][0],) + tables
     )
 
-    def gather(index, shift, *earlier):
+    def gather(indices, shift, *earlier):
         parts = []
         for step in range(blocks):
             block = ((layer ^ step) + (blocks - shift)) % blocks
-            part = lax.select_n(block ^ band, *moved[index])
+            part = jnp.stack([lax.select_n(block ^ band, *moved[index]) for index in indices])
             if earlier:
                 part = after(part, *earlier)
             if step:
@@ -331,7 +336,8 @@
 
     known = {}
     for index in range(count):
-        known[index] = gather(index, 0, *(known[index - 1][1:] if index else ()))
+        earlier = known[index - 1][0][1:] if index else ()
+        known[index] = (gather([index], 0, *earlier), 0)
 
     def exchange(values):
         axes = ("inner", "band")
@@ -374,7 +380,8 @@
             held.update(results)
 
     for index in range(count):
-        known[count + index] = gather(index, 1, *known[count - 1][1:])
+        earlier = () if index else known[count - 1][0][1:]
+        known[count + index] = (gather([index], 1, *earlier), 0)
     steps = schedule(count)
     ends = {step[1:] for step in steps if step.endswith("b")}
     halves_of = []
@@ -392,14 +399,19 @@
             for b in range(blocks)
         ]
 
+    first_moved = []
     results = [(index, 0, held[index]) for index in range(count - 1)]
     results += [(count - 1, half, value) for half, value in enumerate(halves_of)]
     for index, half, result in results:
         result = result.reshape(-1, blocks, piece // 2, rows, columns)
         for step in range(blocks):
             part = lax.dynamic_index_in_dim(result, layer ^ band ^ step, 1, keepdims=False)
+            if half:
+                part = after(part, first_moved[step])
             part = lax.ppermute(part, everywhere, route(step))
             spot = (index, layer ^ step, half, 0, 0, 0)
+            if not (index or half):
+                first_moved.append(part)
             out = lax.dynamic_update_slice(out, part[None, None], spot)
     return out.reshape(count, planes, rows, columns)
 

time: 380 us -> 356 us (0.937); the launches traced: 378 us -> 349 us
  waiting for transfers between devices: 153 us -> 123 us
    ppermute x12, starting transfers between devices: 55.2 us -> 37.3 us  [layered_body(): part = lax.ppermute(part, everywhere, route(step))]
    ppermute x91 -> x105, starting transfers between devices: 93 us -> 111 us  [exchange(): lax.ppermute(value, axes, [(at, at ^ place % group) for at in range(group)])]
    ppermute x91 -> x105, waiting for transfers between devices: 82.4 us -> 65.4 us  [exchange(): lax.ppermute(value, axes, [(at, at ^ place % group) for at in range(group)])]
    ppermute x12, waiting for transfers between devices: 13 us -> 3.59 us  [layered_body(): part = lax.ppermute(part, everywhere, route(step))]
    pallas_call x6 -> x7, Pallas kernels: 6.39 us -> 7.78 us  [forward(): pl.pallas_call(functools.partial(forward_kernel, group, pieces, leads, pl...]
    pallas_call x6 -> x7, Pallas kernels: 7.62 us -> 7.74 us  [through_depth(): pl.pallas_call(functools.partial(depth_kernel, planes, group), grid=(coun...]
  transfers between devices with their start and end apart: 121 -> 135, of which waited for: 35 -> 37; matrix products, arithmetic and copies ran while one was open for 2% -> 2% of each run, Pallas kernels for 6% -> 6%
where the time goes in v1:
time: 356 us; the launch traced here: 349 us
  starting transfers between devices  166 us (47%)
  waiting for transfers between devices  123 us (35%)
  local copies, waits for them, and re-layouts  29.3 us (8%)
  Pallas kernels  22.1 us (6%)
  other arithmetic  6.84 us (2%)
    ppermute x105, starting transfers between devices, exchange(): lax.ppermute(value, axes, [(at, at ^ place % group) for at in range(group)])  111 us
    ppermute x105, waiting for transfers between devices, exchange(): lax.ppermute(value, axes, [(at, at ^ place % group) for at in range(group)])  65.4 us
    ppermute x12, waiting for transfers between devices, gather(): lax.ppermute(part, 'layer', [(at, at ^ step) for at in range(blocks)])  47.7 us
    ppermute x12, starting transfers between devices, layered_body(): part = lax.ppermute(part, everywhere, route(step))  37.3 us
    unnamed x130, local copies, waits for them, and re-layouts  23.5 us
    ppermute x12, starting transfers between devices, gather(): lax.ppermute(part, 'layer', [(at, at ^ step) for at in range(blocks)])  13.2 us
    pallas_call x7, Pallas kernels, forward(): pl.pallas_call(functools.partial(forward_kernel, group, pieces, leads, pl...  7.78 us
    pallas_call x7, Pallas kernels, through_depth(): pl.pallas_call(functools.partial(depth_kernel, planes, group), grid=(coun...  7.74 us
  transfers between devices with their start and end apart: 135, of which 37 were waited for; matrix products, arithmetic and copies ran while one was open for 2% of the time, Pallas kernels for 6%

profile of v1, /device:TPU:0, one launch (start us, length us, event | category | flops | bytes accessed | tf_op | source)
XLA Modules:
  0.0 348.7 jit_solution(4087376380647666617)
XLA Ops:
  2.0 2.4 collective-permute-start.2
  11.4 5.8 %collective-permute-done.1 = f32[4,128,128]{2,1,0:T(8,128)} collective-permute-done((f32[4,128,128]{2,1,0:T(8,128)}, f32[4,128,128]{2,1,0:T(8,128)}, u32[]{:S(2)}, u32[]{:S(2)}) %collective-permute-start.1) | collective-permute-done | bytes 262176 | tf_op jit(solution)/shard_map/ppermute | solution.py:317
  19.3 4.4 %collective-permute-start.5 = (f32[1,4,128,128]{3,2,1,0:T(8,128)}, f32[1,4,128,128]{3,2,1,0:T(8,128)S(1)}, u32[]{:S(2)}, u32[]{:S(2)}) collective-permute-start(f32[1,4,128,128]{3,2,1,0:T(8,128)} %get-tuple-element.343), channel_id=1, source_target_pairs={{0,24},{8,16},{16,8},{24,0},{1,25},{9,17},{17,9},{25,1},{2,26},{10... | collective-permute-start | bytes 786440 | tf_op jit(solution)/shard_map/ppermute | solution.py:333
  27.1 4.1 %collective-permute-done.5.refs_3_.refs_11_ = f32[1,4,128,128]{3,2,1,0:T(8,128)S(1)} collective-permute-done((f32[1,4,128,128]{3,2,1,0:T(8,128)}, f32[1,4,128,128]{3,2,1,0:T(8,128)S(1)}, u32[]{:S(2)}, u32[]{:S(2)}) %collective-permute-start.5) | collective-permute-done | bytes 262176 | tf_op jit(solution)/shard_map/ppermute | solution.py:333
  31.2 15.2 %collective-permute-done.4.refs_2_.refs_10_ = f32[1,4,128,128]{3,2,1,0:T(8,128)S(1)} collective-permute-done((f32[1,4,128,128]{3,2,1,0:T(8,128)}, f32[1,4,128,128]{3,2,1,0:T(8,128)S(1)}, u32[]{:S(2)}, u32[]{:S(2)}) %collective-permute-start.4) | collective-permute-done | bytes 262176 | tf_op jit(solution)/shard_map/ppermute | solution.py:333
  51.2 2.5 collective-permute-start.11
  55.8 2.5 collective-permute-start.18
  58.2 4.7 %collective-permute-done.10.refs_5_ = f32[1,256,128]{2,1,0:T(8,128)S(1)} collective-permute-done((f32[1,256,128]{2,1,0:T(8,128)S(1)}, f32[1,256,128]{2,1,0:T(8,128)S(1)}, u32[]{:S(2)}, u32[]{:S(2)}) %collective-permute-start.10) | collective-permute-done | bytes 131104 | tf_op jit(solution)/shard_map/ppermute | solution.py:345
  67.9 7.3 %collective-permute-done.16.refs_5_.refs_1_.refs_13_.refs_9_ = f32[1,4,128,128]{3,2,1,0:T(8,128)S(1)} collective-permute-done((f32[1,4,128,128]{3,2,1,0:T(8,128)S(1)}, f32[1,4,128,128]{3,2,1,0:T(8,128)S(1)}, u32[]{:S(2)}, u32[]{:S(2)}) %collective-permute-start.16) | collective-permute-done | bytes 262176 | tf_op jit(solution)/shard_map/ppermute | solution.py:333
  76.7 4.2 %collective-permute-done.17.refs_6_.refs_2_.refs_14_.refs_10_ = f32[1,4,128,128]{3,2,1,0:T(8,128)S(1)} collective-permute-done((f32[1,4,128,128]{3,2,1,0:T(8,128)S(1)}, f32[1,4,128,128]{3,2,1,0:T(8,128)S(1)}, u32[]{:S(2)}, u32[]{:S(2)}) %collective-permute-start.17) | collective-permute-done | bytes 262176 | tf_op jit(solution)/shard_map/ppermute | solution.py:333
  87.5 4.3 %collective-permute-done.23.refs_5_ = f32[1,256,128]{2,1,0:T(8,128)S(1)} collective-permute-done((f32[1,256,128]{2,1,0:T(8,128)S(1)}, f32[1,256,128]{2,1,0:T(8,128)S(1)}, u32[]{:S(2)}, u32[]{:S(2)}) %collective-permute-start.23) | collective-permute-done | bytes 131104 | tf_op jit(solution)/shard_map/ppermute | solution.py:345
  99.1 5.9 %collective-permute-done.29.refs_4_ = f32[1,256,128]{2,1,0:T(8,128)S(1)} collective-permute-done((f32[1,256,128]{2,1,0:T(8,128)S(1)}, f32[1,256,128]{2,1,0:T(8,128)S(1)}, u32[]{:S(2)}, u32[]{:S(2)}) %collective-permute-start.29) | collective-permute-done | bytes 131104 | tf_op jit(solution)/shard_map/ppermute | solution.py:345
  112.2 8.8 %collective-permute-done.51.refs_6_.refs_10_ = f32[1,4,128,128]{3,2,1,0:T(8,128)S(1)} collective-permute-done((f32[1,4,128,128]{3,2,1,0:T(8,128)S(1)}, f32[1,4,128,128]{3,2,1,0:T(8,128)S(1)}, u32[]{:S(2)}, u32[]{:S(2)}) %collective-permute-start.51) | collective-permute-done | bytes 262176 | tf_op jit(solution)/shard_map/ppermute | solution.py:333
  127.4 4.9 %collective-permute-done.37.refs_5_ = f32[1,256,128]{2,1,0:T(8,128)S(1)} collective-permute-done((f32[1,256,128]{2,1,0:T(8,128)S(1)}, f32[1,256,128]{2,1,0:T(8,128)S(1)}, u32[]{:S(2)}, u32[]{:S(2)}) %collective-permute-start.37) | collective-permute-done | bytes 131104 | tf_op jit(solution)/shard_map/ppermute | solution.py:345
  132.3 3.0 collective-permute-start.41
  138.3 3.5 %collective-permute-done.45.refs_3_ = f32[1,256,128]{2,1,0:T(8,128)S(1)} collective-permute-done((f32[1,256,128]{2,1,0:T(8,128)S(1)}, f32[1,256,128]{2,1,0:T(8,128)S(1)}, u32[]{:S(2)}, u32[]{:S(2)}) %collective-permute-start.45) | collective-permute-done | bytes 131104 | tf_op jit(solution)/shard_map/ppermute | solution.py:345
  144.4 2.4 collective-permute-done.40.refs_5_.refs_9_
  148.9 4.9 %collective-permute-done.41.refs_6_.refs_10_ = f32[1,4,128,128]{3,2,1,0:T(8,128)S(1)} collective-permute-done((f32[1,4,128,128]{3,2,1,0:T(8,128)S(1)}, f32[1,4,128,128]{3,2,1,0:T(8,128)S(1)}, u32[]{:S(2)}, u32[]{:S(2)}) %collective-permute-start.41) | collective-permute-done | bytes 262176 | tf_op jit(solution)/shard_map/ppermute | solution.py:333
  167.6 5.9 %collective-permute-done.57.refs_5_ = f32[1,256,128]{2,1,0:T(8,128)S(1)} collective-permute-done((f32[1,256,128]{2,1,0:T(8,128)S(1)}, f32[1,256,128]{2,1,0:T(8,128)S(1)}, u32[]{:S(2)}, u32[]{:S(2)}) %collective-permute-start.57) | collective-permute-done | bytes 131104 | tf_op jit(solution)/shard_map/ppermute | solution.py:345
  184.6 5.6 %collective-permute-done.64.refs_5_ = f32[1,256,128]{2,1,0:T(8,128)S(1)} collective-permute-done((f32[1,256,128]{2,1,0:T(8,128)S(1)}, f32[1,256,128]{2,1,0:T(8,128)S(1)}, u32[]{:S(2)}, u32[]{:S(2)}) %collective-permute-start.64) | collective-permute-done | bytes 131104 | tf_op jit(solution)/shard_map/ppermute | solution.py:345
  196.3 4.8 %collective-permute-done.71.refs_5_ = f32[1,256,128]{2,1,0:T(8,128)S(1)} collective-permute-done((f32[1,256,128]{2,1,0:T(8,128)S(1)}, f32[1,256,128]{2,1,0:T(8,128)S(1)}, u32[]{:S(2)}, u32[]{:S(2)}) %collective-permute-start.71) | collective-permute-done | bytes 131104 | tf_op jit(solution)/shard_map/ppermute | solution.py:345
  211.1 5.0 %collective-permute-done.78.refs_5_ = f32[1,256,128]{2,1,0:T(8,128)S(1)} collective-permute-done((f32[1,256,128]{2,1,0:T(8,128)S(1)}, f32[1,256,128]{2,1,0:T(8,128)S(1)}, u32[]{:S(2)}, u32[]{:S(2)}) %collective-permute-start.78) | collective-permute-done | bytes 131104 | tf_op jit(solution)/shard_map/ppermute | solution.py:345
  221.5 2.4 collective-permute-start.94
  225.7 5.2 %collective-permute-done.92.refs_5_ = f32[1,256,128]{2,1,0:T(8,128)S(1)} collective-permute-done((f32[1,256,128]{2,1,0:T(8,128)S(1)}, f32[1,256,128]{2,1,0:T(8,128)S(1)}, u32[]{:S(2)}, u32[]{:S(2)}) %collective-permute-start.92) | collective-permute-done | bytes 131104 | tf_op jit(solution)/shard_map/ppermute | solution.py:345
  248.3 3.1 collective-permute-start.101
  281.8 2.7 collective-permute-done.111.refs_6_
  296.5 2.4 collective-permute-start.98
  302.9 5.2 %collective-permute-start.130 = (f32[1,128,128]{2,1,0:T(8,128)S(1)}, f32[1,128,128]{2,1,0:T(8,128)S(1)}, u32[]{:S(2)}, u32[]{:S(2)}) collective-permute-start(f32[1,128,128]{2,1,0:T(8,128)S(1)} %get-tuple-element.334), channel_id=1, source_target_pairs={{0,7},{1,6},{2,5},{3,4},{4,3},{5,2},{6,1},{7,0},{8,15},{9,14},{10,... | collective-permute-start | bytes 196616 | tf_op jit(solution)/shard_map/ppermute | solution.py:345
  308.1 3.5 %collective-permute-done.130.refs_7_ = f32[1,128,128]{2,1,0:T(8,128)S(1)} collective-permute-done((f32[1,128,128]{2,1,0:T(8,128)S(1)}, f32[1,128,128]{2,1,0:T(8,128)S(1)}, u32[]{:S(2)}, u32[]{:S(2)}) %collective-permute-start.130) | collective-permute-done | bytes 65568 | tf_op jit(solution)/shard_map/ppermute | solution.py:345
  311.6 3.1 collective-permute-start.123
  317.5 11.7 %collective-permute-start.121 = (f32[1,2,128,128]{3,2,1,0:T(8,128)S(1)}, f32[1,2,128,128]{3,2,1,0:T(8,128)S(1)}, u32[]{:S(2)}, u32[]{:S(2)}) collective-permute-start(f32[1,2,128,128]{3,2,1,0:T(8,128)S(1)} %get-tuple-element.372), channel_id=1, source_target_pairs={{0,8},{1,0},{2,24},{3,16},{4,12},{5,4},{6,28},{7,20},{8,9},{9,1},{... | collective-permute-start | bytes 393224 | tf_op jit(solution)/shard_map/ppermute | solution.py:411
  330.3 10.7 %collective-permute-start.133 = (f32[1,2,128,128]{3,2,1,0:T(8,128)S(1)}, f32[1,2,128,128]{3,2,1,0:T(8,128)S(1)}, u32[]{:S(2)}, u32[]{:S(2)}) collective-permute-start(f32[1,2,128,128]{3,2,1,0:T(8,128)S(1)} %get-tuple-element.337), channel_id=1, source_target_pairs={{0,16},{1,24},{2,0},{3,8},{4,20},{5,28},{6,4},{7,12},{8,17},{9,25}... | collective-permute-start | bytes 393224 | tf_op jit(solution)/shard_map/ppermute | solution.py:411
  (428 shorter events, 185.3 us)
Async XLA Ops:
  24.6 21.8 %collective-permute-start.4 = (f32[1,4,128,128]{3,2,1,0:T(8,128)}, f32[1,4,128,128]{3,2,1,0:T(8,128)S(1)}, u32[]{:S(2)}, u32[]{:S(2)}) collective-permute-start(f32[1,4,128,128]{3,2,1,0:T(8,128)} %get-tuple-element.344), channel_id=1, source_target_pairs={{0,16},{8,24},{16,0},{24,8},{1,17},{9,25},{17,1},{25,9},{2,18},{10... | collective-permute-start | bytes 786440 | tf_op jit(solution)/shard_map/ppermute | solution.py:333
  24.6 21.8 %collective-permute-start.3 = (f32[1,4,128,128]{3,2,1,0:T(8,128)}, f32[1,4,128,128]{3,2,1,0:T(8,128)S(1)}, u32[]{:S(2)}, u32[]{:S(2)}) collective-permute-start(f32[1,4,128,128]{3,2,1,0:T(8,128)} %get-tuple-element.345), channel_id=1, source_target_pairs={{0,8},{8,0},{16,24},{24,16},{1,9},{9,1},{17,25},{25,17},{2,10},{10... | collective-permute-start | bytes 786440 | tf_op jit(solution)/shard_map/ppermute | solution.py:333
  25.3 23.7 %collective-permute-start.14 = (f32[4,128,128]{2,1,0:T(8,128)}, f32[4,128,128]{2,1,0:T(8,128)S(1)}, u32[]{:S(2)}, u32[]{:S(2)}) collective-permute-start(f32[4,128,128]{2,1,0:T(8,128)} %get-tuple-element.193), channel_id=1, source_target_pairs={{0,2},{1,3},{2,0},{3,1},{4,6},{5,7},{6,4},{7,5},{8,10},{9,11},{10,... | collective-permute-start | bytes 786440 | tf_op jit(solution)/shard_map/ppermute | solution.py:317
  27.1 22.2 %collective-permute-start.15 = (f32[4,128,128]{2,1,0:T(8,128)}, f32[4,128,128]{2,1,0:T(8,128)S(1)}, u32[]{:S(2)}, u32[]{:S(2)}) collective-permute-start(f32[4,128,128]{2,1,0:T(8,128)} %get-tuple-element.194), channel_id=1, source_target_pairs={{0,3},{1,2},{2,1},{3,0},{4,7},{5,6},{6,5},{7,4},{8,11},{9,10},{10,... | collective-permute-start | bytes 786440 | tf_op jit(solution)/shard_map/ppermute | solution.py:317
  31.2 19.7 %collective-permute-start.13 = (f32[4,128,128]{2,1,0:T(8,128)S(1)}, f32[4,128,128]{2,1,0:T(8,128)S(1)}, u32[]{:S(2)}, u32[]{:S(2)}) collective-permute-start(f32[4,128,128]{2,1,0:T(8,128)S(1)} %get-tuple-element.192), channel_id=1, source_target_pairs={{0,1},{1,0},{2,3},{3,2},{4,5},{5,4},{6,7},{7,6},{8,9},{9,8},{10,11... | collective-permute-start | bytes 786440 | tf_op jit(solution)/shard_map/ppermute | solution.py:317
  58.2 17.0 %collective-permute-start.16 = (f32[1,4,128,128]{3,2,1,0:T(8,128)S(1)}, f32[1,4,128,128]{3,2,1,0:T(8,128)S(1)}, u32[]{:S(2)}, u32[]{:S(2)}) collective-permute-start(f32[1,4,128,128]{3,2,1,0:T(8,128)S(1)} %get-tuple-element.196), channel_id=1, source_target_pairs={{0,8},{8,0},{16,24},{24,16},{1,9},{9,1},{17,25},{25,17},{2,10},{10... | collective-permute-start | bytes 786440 | tf_op jit(solution)/shard_map/ppermute | solution.py:333
  62.9 18.0 %collective-permute-start.17 = (f32[1,4,128,128]{3,2,1,0:T(8,128)S(1)}, f32[1,4,128,128]{3,2,1,0:T(8,128)S(1)}, u32[]{:S(2)}, u32[]{:S(2)}) collective-permute-start(f32[1,4,128,128]{3,2,1,0:T(8,128)S(1)} %get-tuple-element.197), channel_id=1, source_target_pairs={{0,16},{8,24},{16,0},{24,8},{1,17},{9,25},{17,1},{25,9},{2,18},{10... | collective-permute-start | bytes 786440 | tf_op jit(solution)/shard_map/ppermute | solution.py:333
  63.8 18.3 %collective-permute-start.19 = (f32[1,256,128]{2,1,0:T(8,128)S(1)}, f32[1,256,128]{2,1,0:T(8,128)S(1)}, u32[]{:S(2)}, u32[]{:S(2)}) collective-permute-start(f32[1,256,128]{2,1,0:T(8,128)S(1)} %get-tuple-element.203), channel_id=1, source_target_pairs={{0,1},{1,0},{2,3},{3,2},{4,5},{5,4},{6,7},{7,6},{8,9},{9,8},{10,11... | collective-permute-start | bytes 393224 | tf_op jit(solution)/shard_map/ppermute | solution.py:345
  64.6 19.7 %collective-permute-start.20 = (f32[1,256,128]{2,1,0:T(8,128)S(1)}, f32[1,256,128]{2,1,0:T(8,128)S(1)}, u32[]{:S(2)}, u32[]{:S(2)}) collective-permute-start(f32[1,256,128]{2,1,0:T(8,128)S(1)} %get-tuple-element.204), channel_id=1, source_target_pairs={{0,2},{1,3},{2,0},{3,1},{4,6},{5,7},{6,4},{7,5},{8,10},{9,11},{10,... | collective-permute-start | bytes 393224 | tf_op jit(solution)/shard_map/ppermute | solution.py:345
  66.8 19.0 %collective-permute-start.21 = (f32[1,256,128]{2,1,0:T(8,128)S(1)}, f32[1,256,128]{2,1,0:T(8,128)S(1)}, u32[]{:S(2)}, u32[]{:S(2)}) collective-permute-start(f32[1,256,128]{2,1,0:T(8,128)S(1)} %get-tuple-element.205), channel_id=1, source_target_pairs={{0,3},{1,2},{2,1},{3,0},{4,7},{5,6},{6,5},{7,4},{8,11},{9,10},{10,... | collective-permute-start | bytes 393224 | tf_op jit(solution)/shard_map/ppermute | solution.py:345
  105.0 16.0 %collective-permute-start.51 = (f32[1,4,128,128]{3,2,1,0:T(8,128)S(1)}, f32[1,4,128,128]{3,2,1,0:T(8,128)S(1)}, u32[]{:S(2)}, u32[]{:S(2)}) collective-permute-start(f32[1,4,128,128]{3,2,1,0:T(8,128)S(1)} %get-tuple-element.359), channel_id=1, source_target_pairs={{0,16},{8,24},{16,0},{24,8},{1,17},{9,25},{17,1},{25,9},{2,18},{10... | collective-permute-start | bytes 786440 | tf_op jit(solution)/shard_map/ppermute | solution.py:333
  107.2 16.0 %collective-permute-start.34 = (f32[1,256,128]{2,1,0:T(8,128)S(1)}, f32[1,256,128]{2,1,0:T(8,128)S(1)}, u32[]{:S(2)}, u32[]{:S(2)}) collective-permute-start(f32[1,256,128]{2,1,0:T(8,128)S(1)} %get-tuple-element.221), channel_id=1, source_target_pairs={{0,2},{1,3},{2,0},{3,1},{4,6},{5,7},{6,4},{7,5},{8,10},{9,11},{10,... | collective-permute-start | bytes 393224 | tf_op jit(solution)/shard_map/ppermute | solution.py:345
  107.9 16.8 %collective-permute-start.35 = (f32[1,256,128]{2,1,0:T(8,128)S(1)}, f32[1,256,128]{2,1,0:T(8,128)S(1)}, u32[]{:S(2)}, u32[]{:S(2)}) collective-permute-start(f32[1,256,128]{2,1,0:T(8,128)S(1)} %get-tuple-element.222), channel_id=1, source_target_pairs={{0,3},{1,2},{2,1},{3,0},{4,7},{5,6},{6,5},{7,4},{8,11},{9,10},{10,... | collective-permute-start | bytes 393224 | tf_op jit(solution)/shard_map/ppermute | solution.py:345
  110.4 15.6 %collective-permute-start.36 = (f32[1,256,128]{2,1,0:T(8,128)S(1)}, f32[1,256,128]{2,1,0:T(8,128)S(1)}, u32[]{:S(2)}, u32[]{:S(2)}) collective-permute-start(f32[1,256,128]{2,1,0:T(8,128)S(1)} %get-tuple-element.223), channel_id=1, source_target_pairs={{0,4},{1,5},{2,6},{3,7},{4,0},{5,1},{6,2},{7,3},{8,12},{9,13},{10,... | collective-permute-start | bytes 393224 | tf_op jit(solution)/shard_map/ppermute | solution.py:345
  132.3 21.5 %collective-permute-start.41 = (f32[1,4,128,128]{3,2,1,0:T(8,128)S(1)}, f32[1,4,128,128]{3,2,1,0:T(8,128)S(1)}, u32[]{:S(2)}, u32[]{:S(2)}) collective-permute-start(f32[1,4,128,128]{3,2,1,0:T(8,128)S(1)} %get-tuple-element.231), channel_id=1, source_target_pairs={{0,16},{8,24},{16,0},{24,8},{1,17},{9,25},{17,1},{25,9},{2,18},{10... | collective-permute-start | bytes 786440 | tf_op jit(solution)/shard_map/ppermute | solution.py:333
  135.3 19.4 %collective-permute-start.42 = (f32[1,4,128,128]{3,2,1,0:T(8,128)S(1)}, f32[1,4,128,128]{3,2,1,0:T(8,128)S(1)}, u32[]{:S(2)}, u32[]{:S(2)}) collective-permute-start(f32[1,4,128,128]{3,2,1,0:T(8,128)S(1)} %get-tuple-element.232), channel_id=1, source_target_pairs={{0,24},{8,16},{16,8},{24,0},{1,25},{9,17},{17,9},{25,1},{2,26},{10... | collective-permute-start | bytes 786440 | tf_op jit(solution)/shard_map/ppermute | solution.py:333
  141.8 19.5 %collective-permute-start.50 = (f32[1,4,128,128]{3,2,1,0:T(8,128)S(1)}, f32[1,4,128,128]{3,2,1,0:T(8,128)S(1)}, u32[]{:S(2)}, u32[]{:S(2)}) collective-permute-start(f32[1,4,128,128]{3,2,1,0:T(8,128)S(1)} %get-tuple-element.360), channel_id=1, source_target_pairs={{0,8},{8,0},{16,24},{24,16},{1,9},{9,1},{17,25},{25,17},{2,10},{10... | collective-permute-start | bytes 786440 | tf_op jit(solution)/shard_map/ppermute | solution.py:333
  221.5 16.1 %collective-permute-start.94 = (f32[1,256,128]{2,1,0:T(8,128)S(1)}, f32[1,256,128]{2,1,0:T(8,128)S(1)}, u32[]{:S(2)}, u32[]{:S(2)}) collective-permute-start(f32[1,256,128]{2,1,0:T(8,128)S(1)} %get-tuple-element.300), channel_id=1, source_target_pairs={{0,7},{1,6},{2,5},{3,4},{4,3},{5,2},{6,1},{7,0},{8,15},{9,14},{10,... | collective-permute-start | bytes 393224 | tf_op jit(solution)/shard_map/ppermute | solution.py:345
  225.3 15.9 %collective-permute-start.82 = (f32[1,256,128]{2,1,0:T(8,128)S(1)}, f32[1,256,128]{2,1,0:T(8,128)S(1)}, u32[]{:S(2)}, u32[]{:S(2)}) collective-permute-start(f32[1,256,128]{2,1,0:T(8,128)S(1)} %get-tuple-element.286), channel_id=1, source_target_pairs={{0,2},{1,3},{2,0},{3,1},{4,6},{5,7},{6,4},{7,5},{8,10},{9,11},{10,... | collective-permute-start | bytes 393224 | tf_op jit(solution)/shard_map/ppermute | solution.py:345
  248.3 21.6 %collective-permute-start.101 = (f32[1,256,128]{2,1,0:T(8,128)}, f32[1,256,128]{2,1,0:T(8,128)}, u32[]{:S(2)}, u32[]{:S(2)}) collective-permute-start(f32[1,256,128]{2,1,0:T(8,128)} %get-tuple-element.304), channel_id=1, source_target_pairs={{0,3},{1,2},{2,1},{3,0},{4,7},{5,6},{6,5},{7,4},{8,11},{9,10},{10,... | collective-permute-start | bytes 393224 | tf_op jit(solution)/shard_map/ppermute | solution.py:345
  252.1 18.3 %collective-permute-start.102 = (f32[1,256,128]{2,1,0:T(8,128)}, f32[1,256,128]{2,1,0:T(8,128)}, u32[]{:S(2)}, u32[]{:S(2)}) collective-permute-start(f32[1,256,128]{2,1,0:T(8,128)} %get-tuple-element.305), channel_id=1, source_target_pairs={{0,4},{1,5},{2,6},{3,7},{4,0},{5,1},{6,2},{7,3},{8,12},{9,13},{10,... | collective-permute-start | bytes 393224 | tf_op jit(solution)/shard_map/ppermute | solution.py:345
  252.8 17.7 %collective-permute-start.103 = (f32[1,256,128]{2,1,0:T(8,128)}, f32[1,256,128]{2,1,0:T(8,128)}, u32[]{:S(2)}, u32[]{:S(2)}) collective-permute-start(f32[1,256,128]{2,1,0:T(8,128)} %get-tuple-element.306), channel_id=1, source_target_pairs={{0,5},{1,4},{2,7},{3,6},{4,1},{5,0},{6,3},{7,2},{8,13},{9,12},{10,... | collective-permute-start | bytes 393224 | tf_op jit(solution)/shard_map/ppermute | solution.py:345
  255.1 16.8 %collective-permute-start.104 = (f32[1,256,128]{2,1,0:T(8,128)}, f32[1,256,128]{2,1,0:T(8,128)}, u32[]{:S(2)}, u32[]{:S(2)}) collective-permute-start(f32[1,256,128]{2,1,0:T(8,128)} %get-tuple-element.307), channel_id=1, source_target_pairs={{0,6},{1,7},{2,4},{3,5},{4,2},{5,3},{6,0},{7,1},{8,14},{9,15},{10,... | collective-permute-start | bytes 393224 | tf_op jit(solution)/shard_map/ppermute | solution.py:345
  296.5 18.9 %collective-permute-start.98 = (f32[2,2,128,128]{3,2,1,0:T(8,128)S(1)}, f32[2,2,128,128]{3,2,1,0:T(8,128)S(1)}, u32[]{:S(2)}, u32[]{:S(2)}) collective-permute-start(f32[2,2,128,128]{3,2,1,0:T(8,128)S(1)} %get-tuple-element.354), channel_id=1, source_target_pairs={{0,24},{1,16},{2,8},{3,0},{4,28},{5,20},{6,12},{7,4},{8,25},{9,17}... | collective-permute-start | bytes 786440 | tf_op jit(solution)/shard_map/ppermute | solution.py:411
  298.9 18.6 %collective-permute-start.97 = (f32[2,2,128,128]{3,2,1,0:T(8,128)S(1)}, f32[2,2,128,128]{3,2,1,0:T(8,128)S(1)}, u32[]{:S(2)}, u32[]{:S(2)}) collective-permute-start(f32[2,2,128,128]{3,2,1,0:T(8,128)S(1)} %get-tuple-element.355), channel_id=1, source_target_pairs={{0,16},{1,24},{2,0},{3,8},{4,20},{5,28},{6,4},{7,12},{8,17},{9,25}... | collective-permute-start | bytes 786440 | tf_op jit(solution)/shard_map/ppermute | solution.py:411
  301.2 28.0 %collective-permute-start.96 = (f32[2,2,128,128]{3,2,1,0:T(8,128)S(1)}, f32[2,2,128,128]{3,2,1,0:T(8,128)S(1)}, u32[]{:S(2)}, u32[]{:S(2)}) collective-permute-start(f32[2,2,128,128]{3,2,1,0:T(8,128)S(1)} %get-tuple-element.356), channel_id=1, source_target_pairs={{0,8},{1,0},{2,24},{3,16},{4,12},{5,4},{6,28},{7,20},{8,9},{9,1},{... | collective-permute-start | bytes 786440 | tf_op jit(solution)/shard_map/ppermute | solution.py:411
  302.2 27.7 %collective-permute-start.95 = (f32[2,2,128,128]{3,2,1,0:T(8,128)S(1)}, f32[2,2,128,128]{3,2,1,0:T(8,128)S(1)}, u32[]{:S(2)}, u32[]{:S(2)}) collective-permute-start(f32[2,2,128,128]{3,2,1,0:T(8,128)S(1)} %get-tuple-element.357), channel_id=1, source_target_pairs={{0,0},{1,8},{2,16},{3,24},{4,4},{5,12},{6,20},{7,28},{8,1},{9,9},{... | collective-permute-start | bytes 786440 | tf_op jit(solution)/shard_map/ppermute | solution.py:411
  311.6 32.0 %collective-permute-start.123 = (f32[1,2,128,128]{3,2,1,0:T(8,128)S(1)}, f32[1,2,128,128]{3,2,1,0:T(8,128)S(1)}, u32[]{:S(2)}, u32[]{:S(2)}) collective-permute-start(f32[1,2,128,128]{3,2,1,0:T(8,128)S(1)} %get-tuple-element.370), channel_id=1, source_target_pairs={{0,24},{1,16},{2,8},{3,0},{4,28},{5,20},{6,12},{7,4},{8,25},{9,17}... | collective-permute-start | bytes 393224 | tf_op jit(solution)/shard_map/ppermute | solution.py:411
  315.4 27.6 %collective-permute-start.122 = (f32[1,2,128,128]{3,2,1,0:T(8,128)S(1)}, f32[1,2,128,128]{3,2,1,0:T(8,128)S(1)}, u32[]{:S(2)}, u32[]{:S(2)}) collective-permute-start(f32[1,2,128,128]{3,2,1,0:T(8,128)S(1)} %get-tuple-element.371), channel_id=1, source_target_pairs={{0,16},{1,24},{2,0},{3,8},{4,20},{5,28},{6,4},{7,12},{8,17},{9,25}... | collective-permute-start | bytes 393224 | tf_op jit(solution)/shard_map/ppermute | solution.py:411
  317.5 23.6 %collective-permute-start.121 = (f32[1,2,128,128]{3,2,1,0:T(8,128)S(1)}, f32[1,2,128,128]{3,2,1,0:T(8,128)S(1)}, u32[]{:S(2)}, u32[]{:S(2)}) collective-permute-start(f32[1,2,128,128]{3,2,1,0:T(8,128)S(1)} %get-tuple-element.372), channel_id=1, source_target_pairs={{0,8},{1,0},{2,24},{3,16},{4,12},{5,4},{6,28},{7,20},{8,9},{9,1},{... | collective-permute-start | bytes 393224 | tf_op jit(solution)/shard_map/ppermute | solution.py:411
  329.9 17.4 %collective-permute-start.134 = (f32[1,2,128,128]{3,2,1,0:T(8,128)S(1)}, f32[1,2,128,128]{3,2,1,0:T(8,128)S(1)}, u32[]{:S(2)}, u32[]{:S(2)}) collective-permute-start(f32[1,2,128,128]{3,2,1,0:T(8,128)S(1)} %get-tuple-element.338), channel_id=1, source_target_pairs={{0,24},{1,16},{2,8},{3,0},{4,28},{5,20},{6,12},{7,4},{8,25},{9,17}... | collective-permute-start | bytes 393224 | tf_op jit(solution)/shard_map/ppermute | solution.py:411
  330.3 17.0 %collective-permute-start.133 = (f32[1,2,128,128]{3,2,1,0:T(8,128)S(1)}, f32[1,2,128,128]{3,2,1,0:T(8,128)S(1)}, u32[]{:S(2)}, u32[]{:S(2)}) collective-permute-start(f32[1,2,128,128]{3,2,1,0:T(8,128)S(1)} %get-tuple-element.337), channel_id=1, source_target_pairs={{0,16},{1,24},{2,0},{3,8},{4,20},{5,28},{6,4},{7,12},{8,17},{9,25}... | collective-permute-start | bytes 393224 | tf_op jit(solution)/shard_map/ppermute | solution.py:411
  (168 other events, 2109.5 us)

commit v2 on v1

--- a/solution.py
+++ b/solution.py
@@ -309,7 +309,7 @@
         source = after(split, across) if index else split
         for step in range(blocks):
             part = lax.dynamic_slice(
-                source, (index, band ^ step, 0, 0, 0), (1, 1, piece, rows, columns)
+                source if step else after(split, across), (index, band ^ step, 0, 0, 0), (1, 1, piece, rows, columns)
             ).reshape(piece, rows, columns)
             if step:
                 if index:
@@ -324,10 +324,13 @@
 
     def gather(indices, shift, *earlier):
         parts = []
+        sources = {index: moved[index] for index in indices}
+        if shift:
+            sources = {index: lax.optimization_barrier((moved[index], known[0][0][1]))[0] for index in indices}
         for step in range(blocks):
             block = ((layer ^ step) + (blocks - shift)) % blocks
-            part = jnp.stack([lax.select_n(block ^ band, *moved[index]) for index in indices])
-            if earlier:
+            part = jnp.stack([lax.select_n(block ^ band, *sources[index]) for index in indices])
+            if earlier and step:
                 part = after(part, *earlier)
             if step:
                 part = lax.ppermute(part, "layer", [(at, at ^ step) for at in range(blocks)])
@@ -340,13 +343,14 @@
         known[index] = (gather([index], 0, *earlier), 0)
 
     def exchange(values):
-        axes = ("inner", "band")
-        return [
-            lax.ppermute(value, axes, [(at, at ^ place % group) for at in range(group)])
-            if place % group
-            else value
-            for place, value in enumerate(values)
-        ]
+        moved = []
+        for place, value in enumerate(values):
+            step = place % group
+            if step:
+                pairs = [(at, at ^ step) for at in range(group)]
+                value = lax.ppermute(value, ("inner", "band"), pairs)
+            moved.append(value)
+        return moved
 
     batches = batch_list(count)
     held, state = {}, {}

time: 356 us -> 355 us (level)
  waiting for transfers between devices: 123 us -> 117 us
    ppermute x105, waiting for transfers between devices: 65.4 us -> 60.8 us  [exchange(): value = lax.ppermute(value, ('inner', 'band'), pairs)]
    ppermute x12, starting transfers between devices: 13.2 us -> 17.1 us  [gather(): lax.ppermute(part, 'layer', [(at, at ^ step) for at in range(blocks)])]
    unnamed x130 -> x200, local copies, waits for them, and re-layouts: 23.5 us -> 26.2 us
  transfers between devices with their start and end apart: 135 -> 135, of which waited for: 37 -> 32; matrix products, arithmetic and copies ran while one was open for 2% -> 3% of each run, Pallas kernels for 6% -> 7%
where the time goes in v2:
time: 355 us; the launch traced here: 348 us
  starting transfers between devices  167 us (47%)
  waiting for transfers between devices  117 us (33%)
  local copies, waits for them, and re-layouts  32.4 us (9%)
  Pallas kernels  25.3 us (7%)
  other arithmetic  6.09 us (2%)
    ppermute x105, starting transfers between devices, exchange(): value = lax.ppermute(value, ('inner', 'band'), pairs)  108 us
    ppermute x105, waiting for transfers between devices, exchange(): value = lax.ppermute(value, ('inner', 'band'), pairs)  60.8 us
    ppermute x12, waiting for transfers between devices, gather(): lax.ppermute(part, 'layer', [(at, at ^ step) for at in range(blocks)])  45.9 us
    ppermute x12, starting transfers between devices, layered_body(): part = lax.ppermute(part, everywhere, route(step))  36.8 us
    unnamed x200, local copies, waits for them, and re-layouts  26.2 us
    ppermute x12, starting transfers between devices, gather(): lax.ppermute(part, 'layer', [(at, at ^ step) for at in range(blocks)])  17.1 us
    pallas_call x7, Pallas kernels, through_depth(): pl.pallas_call(functools.partial(depth_kernel, planes, group), grid=(coun...  9.48 us
    pallas_call x7, Pallas kernels, forward(): pl.pallas_call(functools.partial(forward_kernel, group, pieces, leads, pl...  8.24 us
  transfers between devices with their start and end apart: 135, of which 32 were waited for; matrix products, arithmetic and copies ran while one was open for 3% of the time, Pallas kernels for 7%

profile of v2, /device:TPU:0, one launch (start us, length us, event | category | flops | bytes accessed | tf_op | source)
XLA Modules:
  0.0 348.5 jit_solution(11037005687511221188)
XLA Ops:
  2.5 2.6 collective-permute-start.2
  12.2 5.7 %collective-permute-done.1 = f32[4,128,128]{2,1,0:T(8,128)S(1)} collective-permute-done((f32[4,128,128]{2,1,0:T(8,128)}, f32[4,128,128]{2,1,0:T(8,128)S(1)}, u32[]{:S(2)}, u32[]{:S(2)}) %collective-permute-start.1) | collective-permute-done | bytes 262176 | tf_op jit(solution)/shard_map/ppermute | solution.py:317
  18.9 3.8 %collective-permute-start.5 = (f32[1,4,128,128]{3,2,1,0:T(8,128)S(1)}, f32[1,4,128,128]{3,2,1,0:T(8,128)S(1)}, u32[]{:S(2)}, u32[]{:S(2)}) collective-permute-start(f32[1,4,128,128]{3,2,1,0:T(8,128)S(1)} %get-tuple-element.351), channel_id=1, source_target_pairs={{0,24},{8,16},{16,8},{24,0},{1,25},{9,17},{17,9},{25,1},{2,26},{10... | collective-permute-start | bytes 786440 | tf_op jit(solution)/shard_map/ppermute | solution.py:336
  25.5 4.6 %collective-permute-done.5.refs_3_.refs_11_ = f32[1,4,128,128]{3,2,1,0:T(8,128)S(1)} collective-permute-done((f32[1,4,128,128]{3,2,1,0:T(8,128)S(1)}, f32[1,4,128,128]{3,2,1,0:T(8,128)S(1)}, u32[]{:S(2)}, u32[]{:S(2)}) %collective-permute-start.5) | collective-permute-done | bytes 262176 | tf_op jit(solution)/shard_map/ppermute | solution.py:336
  30.2 14.5 %collective-permute-done.4.refs_2_.refs_10_ = f32[1,4,128,128]{3,2,1,0:T(8,128)S(1)} collective-permute-done((f32[1,4,128,128]{3,2,1,0:T(8,128)S(1)}, f32[1,4,128,128]{3,2,1,0:T(8,128)S(1)}, u32[]{:S(2)}, u32[]{:S(2)}) %collective-permute-start.4) | collective-permute-done | bytes 262176 | tf_op jit(solution)/shard_map/ppermute | solution.py:336
  49.5 2.6 collective-permute-done.7.refs_2_
  53.9 2.5 collective-permute-start.18
  56.4 2.4 collective-permute-start.11
  59.0 4.4 %collective-permute-done.11.refs_6_ = f32[1,256,128]{2,1,0:T(8,128)S(1)} collective-permute-done((f32[1,256,128]{2,1,0:T(8,128)S(1)}, f32[1,256,128]{2,1,0:T(8,128)S(1)}, u32[]{:S(2)}, u32[]{:S(2)}) %collective-permute-start.11) | collective-permute-done | bytes 131104 | tf_op jit(solution)/shard_map/ppermute | solution.py:351
  69.1 4.3 %collective-permute-done.17.refs_6_.refs_2_.refs_14_.refs_10_ = f32[1,4,128,128]{3,2,1,0:T(8,128)S(1)} collective-permute-done((f32[1,4,128,128]{3,2,1,0:T(8,128)S(1)}, f32[1,4,128,128]{3,2,1,0:T(8,128)S(1)}, u32[]{:S(2)}, u32[]{:S(2)}) %collective-permute-start.17) | collective-permute-done | bytes 262176 | tf_op jit(solution)/shard_map/ppermute | solution.py:336
  88.9 2.6 collective-permute-start.31
  93.9 2.5 collective-permute-start.52
  106.6 14.6 %collective-permute-done.51.refs_6_.refs_10_ = f32[1,4,128,128]{3,2,1,0:T(8,128)S(1)} collective-permute-done((f32[1,4,128,128]{3,2,1,0:T(8,128)S(1)}, f32[1,4,128,128]{3,2,1,0:T(8,128)S(1)}, u32[]{:S(2)}, u32[]{:S(2)}) %collective-permute-start.51) | collective-permute-done | bytes 262176 | tf_op jit(solution)/shard_map/ppermute | solution.py:336
  126.4 6.0 %collective-permute-done.37.refs_5_ = f32[1,256,128]{2,1,0:T(8,128)S(1)} collective-permute-done((f32[1,256,128]{2,1,0:T(8,128)S(1)}, f32[1,256,128]{2,1,0:T(8,128)S(1)}, u32[]{:S(2)}, u32[]{:S(2)}) %collective-permute-start.37) | collective-permute-done | bytes 131104 | tf_op jit(solution)/shard_map/ppermute | solution.py:351
  132.4 3.0 collective-permute-start.41
  138.2 4.1 %collective-permute-done.45.refs_3_ = f32[1,256,128]{2,1,0:T(8,128)S(1)} collective-permute-done((f32[1,256,128]{2,1,0:T(8,128)S(1)}, f32[1,256,128]{2,1,0:T(8,128)S(1)}, u32[]{:S(2)}, u32[]{:S(2)}) %collective-permute-start.45) | collective-permute-done | bytes 131104 | tf_op jit(solution)/shard_map/ppermute | solution.py:351
  144.3 2.5 collective-permute-done.40.refs_5_.refs_9_
  148.5 5.4 %collective-permute-done.41.refs_6_.refs_10_ = f32[1,4,128,128]{3,2,1,0:T(8,128)S(1)} collective-permute-done((f32[1,4,128,128]{3,2,1,0:T(8,128)S(1)}, f32[1,4,128,128]{3,2,1,0:T(8,128)S(1)}, u32[]{:S(2)}, u32[]{:S(2)}) %collective-permute-start.41) | collective-permute-done | bytes 262176 | tf_op jit(solution)/shard_map/ppermute | solution.py:336
  167.3 5.9 %collective-permute-done.57.refs_5_ = f32[1,256,128]{2,1,0:T(8,128)S(1)} collective-permute-done((f32[1,256,128]{2,1,0:T(8,128)S(1)}, f32[1,256,128]{2,1,0:T(8,128)S(1)}, u32[]{:S(2)}, u32[]{:S(2)}) %collective-permute-start.57) | collective-permute-done | bytes 131104 | tf_op jit(solution)/shard_map/ppermute | solution.py:351
  184.8 5.1 %collective-permute-done.64.refs_5_ = f32[1,256,128]{2,1,0:T(8,128)S(1)} collective-permute-done((f32[1,256,128]{2,1,0:T(8,128)S(1)}, f32[1,256,128]{2,1,0:T(8,128)S(1)}, u32[]{:S(2)}, u32[]{:S(2)}) %collective-permute-start.64) | collective-permute-done | bytes 131104 | tf_op jit(solution)/shard_map/ppermute | solution.py:351
  196.5 4.4 %collective-permute-done.71.refs_5_ = f32[1,256,128]{2,1,0:T(8,128)S(1)} collective-permute-done((f32[1,256,128]{2,1,0:T(8,128)S(1)}, f32[1,256,128]{2,1,0:T(8,128)S(1)}, u32[]{:S(2)}, u32[]{:S(2)}) %collective-permute-start.71) | collective-permute-done | bytes 131104 | tf_op jit(solution)/shard_map/ppermute | solution.py:351
  210.8 5.1 %collective-permute-done.78.refs_5_ = f32[1,256,128]{2,1,0:T(8,128)S(1)} collective-permute-done((f32[1,256,128]{2,1,0:T(8,128)S(1)}, f32[1,256,128]{2,1,0:T(8,128)S(1)}, u32[]{:S(2)}, u32[]{:S(2)}) %collective-permute-start.78) | collective-permute-done | bytes 131104 | tf_op jit(solution)/shard_map/ppermute | solution.py:351
  221.2 2.5 collective-permute-start.94
  224.9 4.7 %collective-permute-start.82 = (f32[1,256,128]{2,1,0:T(8,128)S(1)}, f32[1,256,128]{2,1,0:T(8,128)S(1)}, u32[]{:S(2)}, u32[]{:S(2)}) collective-permute-start(f32[1,256,128]{2,1,0:T(8,128)S(1)} %get-tuple-element.298), channel_id=1, source_target_pairs={{0,2},{1,3},{2,0},{3,1},{4,6},{5,7},{6,4},{7,5},{8,10},{9,11},{10,... | collective-permute-start | bytes 393224 | tf_op jit(solution)/shard_map/ppermute | solution.py:351
  245.9 3.3 collective-permute-done.85.refs_5_
  280.6 2.6 collective-permute-done.111.refs_6_
  296.1 3.0 collective-permute-start.98
  302.4 5.2 %collective-permute-start.130 = (f32[1,128,128]{2,1,0:T(8,128)S(1)}, f32[1,128,128]{2,1,0:T(8,128)S(1)}, u32[]{:S(2)}, u32[]{:S(2)}) collective-permute-start(f32[1,128,128]{2,1,0:T(8,128)S(1)} %get-tuple-element.346), channel_id=1, source_target_pairs={{0,7},{1,6},{2,5},{3,4},{4,3},{5,2},{6,1},{7,0},{8,15},{9,14},{10,... | collective-permute-start | bytes 196616 | tf_op jit(solution)/shard_map/ppermute | solution.py:351
  307.6 3.5 %collective-permute-done.130.refs_7_ = f32[1,128,128]{2,1,0:T(8,128)S(1)} collective-permute-done((f32[1,128,128]{2,1,0:T(8,128)S(1)}, f32[1,128,128]{2,1,0:T(8,128)S(1)}, u32[]{:S(2)}, u32[]{:S(2)}) %collective-permute-start.130) | collective-permute-done | bytes 65568 | tf_op jit(solution)/shard_map/ppermute | solution.py:351
  311.2 3.1 collective-permute-start.123
  317.3 11.1 %collective-permute-start.121 = (f32[1,2,128,128]{3,2,1,0:T(8,128)S(1)}, f32[1,2,128,128]{3,2,1,0:T(8,128)S(1)}, u32[]{:S(2)}, u32[]{:S(2)}) collective-permute-start(f32[1,2,128,128]{3,2,1,0:T(8,128)S(1)} %get-tuple-element.385), channel_id=1, source_target_pairs={{0,8},{1,0},{2,24},{3,16},{4,12},{5,4},{6,28},{7,20},{8,9},{9,1},{... | collective-permute-start | bytes 393224 | tf_op jit(solution)/shard_map/ppermute | solution.py:415
  329.5 11.4 %collective-permute-start.133 = (f32[1,2,128,128]{3,2,1,0:T(8,128)S(1)}, f32[1,2,128,128]{3,2,1,0:T(8,128)S(1)}, u32[]{:S(2)}, u32[]{:S(2)}) collective-permute-start(f32[1,2,128,128]{3,2,1,0:T(8,128)S(1)} %get-tuple-element.349), channel_id=1, source_target_pairs={{0,16},{1,24},{2,0},{3,8},{4,20},{5,28},{6,4},{7,12},{8,17},{9,25}... | collective-permute-start | bytes 393224 | tf_op jit(solution)/shard_map/ppermute | solution.py:415
  (499 shorter events, 188.2 us)
Async XLA Ops:
  22.8 21.8 %collective-permute-start.4 = (f32[1,4,128,128]{3,2,1,0:T(8,128)S(1)}, f32[1,4,128,128]{3,2,1,0:T(8,128)S(1)}, u32[]{:S(2)}, u32[]{:S(2)}) collective-permute-start(f32[1,4,128,128]{3,2,1,0:T(8,128)S(1)} %get-tuple-element.376), channel_id=1, source_target_pairs={{0,16},{8,24},{16,0},{24,8},{1,17},{9,25},{17,1},{25,9},{2,18},{10... | collective-permute-start | bytes 786440 | tf_op jit(solution)/shard_map/ppermute | solution.py:336
  22.9 21.7 %collective-permute-start.3 = (f32[1,4,128,128]{3,2,1,0:T(8,128)S(1)}, f32[1,4,128,128]{3,2,1,0:T(8,128)S(1)}, u32[]{:S(2)}, u32[]{:S(2)}) collective-permute-start(f32[1,4,128,128]{3,2,1,0:T(8,128)S(1)} %get-tuple-element.377), channel_id=1, source_target_pairs={{0,8},{8,0},{16,24},{24,16},{1,9},{9,1},{17,25},{25,17},{2,10},{10... | collective-permute-start | bytes 786440 | tf_op jit(solution)/shard_map/ppermute | solution.py:336
  24.0 23.3 %collective-permute-start.14 = (f32[4,128,128]{2,1,0:T(8,128)S(1)}, f32[4,128,128]{2,1,0:T(8,128)S(1)}, u32[]{:S(2)}, u32[]{:S(2)}) collective-permute-start(f32[4,128,128]{2,1,0:T(8,128)S(1)} %get-tuple-element.199), channel_id=1, source_target_pairs={{0,2},{1,3},{2,0},{3,1},{4,6},{5,7},{6,4},{7,5},{8,10},{9,11},{10,... | collective-permute-start | bytes 786440 | tf_op jit(solution)/shard_map/ppermute | solution.py:317
  25.5 22.0 %collective-permute-start.15 = (f32[4,128,128]{2,1,0:T(8,128)S(1)}, f32[4,128,128]{2,1,0:T(8,128)S(1)}, u32[]{:S(2)}, u32[]{:S(2)}) collective-permute-start(f32[4,128,128]{2,1,0:T(8,128)S(1)} %get-tuple-element.200), channel_id=1, source_target_pairs={{0,3},{1,2},{2,1},{3,0},{4,7},{5,6},{6,5},{7,4},{8,11},{9,10},{10,... | collective-permute-start | bytes 786440 | tf_op jit(solution)/shard_map/ppermute | solution.py:317
  30.1 19.0 %collective-permute-start.13 = (f32[4,128,128]{2,1,0:T(8,128)S(1)}, f32[4,128,128]{2,1,0:T(8,128)S(1)}, u32[]{:S(2)}, u32[]{:S(2)}) collective-permute-start(f32[4,128,128]{2,1,0:T(8,128)S(1)} %get-tuple-element.198), channel_id=1, source_target_pairs={{0,1},{1,0},{2,3},{3,2},{4,5},{5,4},{6,7},{7,6},{8,9},{9,8},{10,11... | collective-permute-start | bytes 786440 | tf_op jit(solution)/shard_map/ppermute | solution.py:317
  49.4 19.7 %collective-permute-start.16 = (f32[1,4,128,128]{3,2,1,0:T(8,128)S(1)}, f32[1,4,128,128]{3,2,1,0:T(8,128)S(1)}, u32[]{:S(2)}, u32[]{:S(2)}) collective-permute-start(f32[1,4,128,128]{3,2,1,0:T(8,128)S(1)} %get-tuple-element.201), channel_id=1, source_target_pairs={{0,8},{8,0},{16,24},{24,16},{1,9},{9,1},{17,25},{25,17},{2,10},{10... | collective-permute-start | bytes 786440 | tf_op jit(solution)/shard_map/ppermute | solution.py:336
  52.1 21.3 %collective-permute-start.17 = (f32[1,4,128,128]{3,2,1,0:T(8,128)S(1)}, f32[1,4,128,128]{3,2,1,0:T(8,128)S(1)}, u32[]{:S(2)}, u32[]{:S(2)}) collective-permute-start(f32[1,4,128,128]{3,2,1,0:T(8,128)S(1)} %get-tuple-element.202), channel_id=1, source_target_pairs={{0,16},{8,24},{16,0},{24,8},{1,17},{9,25},{17,1},{25,9},{2,18},{10... | collective-permute-start | bytes 786440 | tf_op jit(solution)/shard_map/ppermute | solution.py:336
  53.9 21.1 %collective-permute-start.18 = (f32[1,4,128,128]{3,2,1,0:T(8,128)S(1)}, f32[1,4,128,128]{3,2,1,0:T(8,128)S(1)}, u32[]{:S(2)}, u32[]{:S(2)}) collective-permute-start(f32[1,4,128,128]{3,2,1,0:T(8,128)S(1)} %get-tuple-element.203), channel_id=1, source_target_pairs={{0,24},{8,16},{16,8},{24,0},{1,25},{9,17},{17,9},{25,1},{2,26},{10... | collective-permute-start | bytes 786440 | tf_op jit(solution)/shard_map/ppermute | solution.py:336
  96.4 24.8 %collective-permute-start.51 = (f32[1,4,128,128]{3,2,1,0:T(8,128)S(1)}, f32[1,4,128,128]{3,2,1,0:T(8,128)S(1)}, u32[]{:S(2)}, u32[]{:S(2)}) collective-permute-start(f32[1,4,128,128]{3,2,1,0:T(8,128)S(1)} %get-tuple-element.365), channel_id=1, source_target_pairs={{0,16},{8,24},{16,0},{24,8},{1,17},{9,25},{17,1},{25,9},{2,18},{10... | collective-permute-start | bytes 786440 | tf_op jit(solution)/shard_map/ppermute | solution.py:336
  99.7 21.9 %collective-permute-start.33 = (f32[1,256,128]{2,1,0:T(8,128)S(1)}, f32[1,256,128]{2,1,0:T(8,128)S(1)}, u32[]{:S(2)}, u32[]{:S(2)}) collective-permute-start(f32[1,256,128]{2,1,0:T(8,128)S(1)} %get-tuple-element.225), channel_id=1, source_target_pairs={{0,1},{1,0},{2,3},{3,2},{4,5},{5,4},{6,7},{7,6},{8,9},{9,8},{10,11... | collective-permute-start | bytes 393224 | tf_op jit(solution)/shard_map/ppermute | solution.py:351
  99.8 23.2 %collective-permute-start.34 = (f32[1,256,128]{2,1,0:T(8,128)S(1)}, f32[1,256,128]{2,1,0:T(8,128)S(1)}, u32[]{:S(2)}, u32[]{:S(2)}) collective-permute-start(f32[1,256,128]{2,1,0:T(8,128)S(1)} %get-tuple-element.226), channel_id=1, source_target_pairs={{0,2},{1,3},{2,0},{3,1},{4,6},{5,7},{6,4},{7,5},{8,10},{9,11},{10,... | collective-permute-start | bytes 393224 | tf_op jit(solution)/shard_map/ppermute | solution.py:351
  100.9 23.5 %collective-permute-start.35 = (f32[1,256,128]{2,1,0:T(8,128)S(1)}, f32[1,256,128]{2,1,0:T(8,128)S(1)}, u32[]{:S(2)}, u32[]{:S(2)}) collective-permute-start(f32[1,256,128]{2,1,0:T(8,128)S(1)} %get-tuple-element.227), channel_id=1, source_target_pairs={{0,3},{1,2},{2,1},{3,0},{4,7},{5,6},{6,5},{7,4},{8,11},{9,10},{10,... | collective-permute-start | bytes 393224 | tf_op jit(solution)/shard_map/ppermute | solution.py:351
  105.5 19.3 %collective-permute-start.36 = (f32[1,256,128]{2,1,0:T(8,128)S(1)}, f32[1,256,128]{2,1,0:T(8,128)S(1)}, u32[]{:S(2)}, u32[]{:S(2)}) collective-permute-start(f32[1,256,128]{2,1,0:T(8,128)S(1)} %get-tuple-element.228), channel_id=1, source_target_pairs={{0,4},{1,5},{2,6},{3,7},{4,0},{5,1},{6,2},{7,3},{8,12},{9,13},{10,... | collective-permute-start | bytes 393224 | tf_op jit(solution)/shard_map/ppermute | solution.py:351
  132.4 21.5 %collective-permute-start.41 = (f32[1,4,128,128]{3,2,1,0:T(8,128)S(1)}, f32[1,4,128,128]{3,2,1,0:T(8,128)S(1)}, u32[]{:S(2)}, u32[]{:S(2)}) collective-permute-start(f32[1,4,128,128]{3,2,1,0:T(8,128)S(1)} %get-tuple-element.239), channel_id=1, source_target_pairs={{0,16},{8,24},{16,0},{24,8},{1,17},{9,25},{17,1},{25,9},{2,18},{10... | collective-permute-start | bytes 786440 | tf_op jit(solution)/shard_map/ppermute | solution.py:336
  135.4 19.6 %collective-permute-start.42 = (f32[1,4,128,128]{3,2,1,0:T(8,128)S(1)}, f32[1,4,128,128]{3,2,1,0:T(8,128)S(1)}, u32[]{:S(2)}, u32[]{:S(2)}) collective-permute-start(f32[1,4,128,128]{3,2,1,0:T(8,128)S(1)} %get-tuple-element.240), channel_id=1, source_target_pairs={{0,24},{8,16},{16,8},{24,0},{1,25},{9,17},{17,9},{25,1},{2,26},{10... | collective-permute-start | bytes 786440 | tf_op jit(solution)/shard_map/ppermute | solution.py:336
  142.3 18.7 %collective-permute-start.50 = (f32[1,4,128,128]{3,2,1,0:T(8,128)S(1)}, f32[1,4,128,128]{3,2,1,0:T(8,128)S(1)}, u32[]{:S(2)}, u32[]{:S(2)}) collective-permute-start(f32[1,4,128,128]{3,2,1,0:T(8,128)S(1)} %get-tuple-element.366), channel_id=1, source_target_pairs={{0,8},{8,0},{16,24},{24,16},{1,9},{9,1},{17,25},{25,17},{2,10},{10... | collective-permute-start | bytes 786440 | tf_op jit(solution)/shard_map/ppermute | solution.py:336
  221.2 16.2 %collective-permute-start.94 = (f32[1,256,128]{2,1,0:T(8,128)S(1)}, f32[1,256,128]{2,1,0:T(8,128)S(1)}, u32[]{:S(2)}, u32[]{:S(2)}) collective-permute-start(f32[1,256,128]{2,1,0:T(8,128)S(1)} %get-tuple-element.312), channel_id=1, source_target_pairs={{0,7},{1,6},{2,5},{3,4},{4,3},{5,2},{6,1},{7,0},{8,15},{9,14},{10,... | collective-permute-start | bytes 393224 | tf_op jit(solution)/shard_map/ppermute | solution.py:351
  224.9 16.4 %collective-permute-start.82 = (f32[1,256,128]{2,1,0:T(8,128)S(1)}, f32[1,256,128]{2,1,0:T(8,128)S(1)}, u32[]{:S(2)}, u32[]{:S(2)}) collective-permute-start(f32[1,256,128]{2,1,0:T(8,128)S(1)} %get-tuple-element.298), channel_id=1, source_target_pairs={{0,2},{1,3},{2,0},{3,1},{4,6},{5,7},{6,4},{7,5},{8,10},{9,11},{10,... | collective-permute-start | bytes 393224 | tf_op jit(solution)/shard_map/ppermute | solution.py:351
  249.8 19.1 %collective-permute-start.101 = (f32[1,256,128]{2,1,0:T(8,128)}, f32[1,256,128]{2,1,0:T(8,128)}, u32[]{:S(2)}, u32[]{:S(2)}) collective-permute-start(f32[1,256,128]{2,1,0:T(8,128)} %get-tuple-element.316), channel_id=1, source_target_pairs={{0,3},{1,2},{2,1},{3,0},{4,7},{5,6},{6,5},{7,4},{8,11},{9,10},{10,... | collective-permute-start | bytes 393224 | tf_op jit(solution)/shard_map/ppermute | solution.py:351
  251.3 17.7 %collective-permute-start.102 = (f32[1,256,128]{2,1,0:T(8,128)}, f32[1,256,128]{2,1,0:T(8,128)}, u32[]{:S(2)}, u32[]{:S(2)}) collective-permute-start(f32[1,256,128]{2,1,0:T(8,128)} %get-tuple-element.317), channel_id=1, source_target_pairs={{0,4},{1,5},{2,6},{3,7},{4,0},{5,1},{6,2},{7,3},{8,12},{9,13},{10,... | collective-permute-start | bytes 393224 | tf_op jit(solution)/shard_map/ppermute | solution.py:351
  252.1 18.2 %collective-permute-start.103 = (f32[1,256,128]{2,1,0:T(8,128)}, f32[1,256,128]{2,1,0:T(8,128)}, u32[]{:S(2)}, u32[]{:S(2)}) collective-permute-start(f32[1,256,128]{2,1,0:T(8,128)} %get-tuple-element.318), channel_id=1, source_target_pairs={{0,5},{1,4},{2,7},{3,6},{4,1},{5,0},{6,3},{7,2},{8,13},{9,12},{10,... | collective-permute-start | bytes 393224 | tf_op jit(solution)/shard_map/ppermute | solution.py:351
  253.9 17.0 %collective-permute-start.104 = (f32[1,256,128]{2,1,0:T(8,128)}, f32[1,256,128]{2,1,0:T(8,128)}, u32[]{:S(2)}, u32[]{:S(2)}) collective-permute-start(f32[1,256,128]{2,1,0:T(8,128)} %get-tuple-element.319), channel_id=1, source_target_pairs={{0,6},{1,7},{2,4},{3,5},{4,2},{5,3},{6,0},{7,1},{8,14},{9,15},{10,... | collective-permute-start | bytes 393224 | tf_op jit(solution)/shard_map/ppermute | solution.py:351
  256.4 15.7 %collective-permute-start.105 = (f32[1,256,128]{2,1,0:T(8,128)}, f32[1,256,128]{2,1,0:T(8,128)}, u32[]{:S(2)}, u32[]{:S(2)}) collective-permute-start(f32[1,256,128]{2,1,0:T(8,128)} %get-tuple-element.320), channel_id=1, source_target_pairs={{0,7},{1,6},{2,5},{3,4},{4,3},{5,2},{6,1},{7,0},{8,15},{9,14},{10,... | collective-permute-start | bytes 393224 | tf_op jit(solution)/shard_map/ppermute | solution.py:351
  296.1 18.8 %collective-permute-start.98 = (f32[2,2,128,128]{3,2,1,0:T(8,128)S(1)}, f32[2,2,128,128]{3,2,1,0:T(8,128)S(1)}, u32[]{:S(2)}, u32[]{:S(2)}) collective-permute-start(f32[2,2,128,128]{3,2,1,0:T(8,128)S(1)} %get-tuple-element.360), channel_id=1, source_target_pairs={{0,24},{1,16},{2,8},{3,0},{4,28},{5,20},{6,12},{7,4},{8,25},{9,17}... | collective-permute-start | bytes 786440 | tf_op jit(solution)/shard_map/ppermute | solution.py:415
  299.1 18.2 %collective-permute-start.97 = (f32[2,2,128,128]{3,2,1,0:T(8,128)S(1)}, f32[2,2,128,128]{3,2,1,0:T(8,128)S(1)}, u32[]{:S(2)}, u32[]{:S(2)}) collective-permute-start(f32[2,2,128,128]{3,2,1,0:T(8,128)S(1)} %get-tuple-element.361), channel_id=1, source_target_pairs={{0,16},{1,24},{2,0},{3,8},{4,20},{5,28},{6,4},{7,12},{8,17},{9,25}... | collective-permute-start | bytes 786440 | tf_op jit(solution)/shard_map/ppermute | solution.py:415
  300.7 27.6 %collective-permute-start.96 = (f32[2,2,128,128]{3,2,1,0:T(8,128)S(1)}, f32[2,2,128,128]{3,2,1,0:T(8,128)S(1)}, u32[]{:S(2)}, u32[]{:S(2)}) collective-permute-start(f32[2,2,128,128]{3,2,1,0:T(8,128)S(1)} %get-tuple-element.362), channel_id=1, source_target_pairs={{0,8},{1,0},{2,24},{3,16},{4,12},{5,4},{6,28},{7,20},{8,9},{9,1},{... | collective-permute-start | bytes 786440 | tf_op jit(solution)/shard_map/ppermute | solution.py:415
  301.8 27.3 %collective-permute-start.95 = (f32[2,2,128,128]{3,2,1,0:T(8,128)S(1)}, f32[2,2,128,128]{3,2,1,0:T(8,128)S(1)}, u32[]{:S(2)}, u32[]{:S(2)}) collective-permute-start(f32[2,2,128,128]{3,2,1,0:T(8,128)S(1)} %get-tuple-element.363), channel_id=1, source_target_pairs={{0,0},{1,8},{2,16},{3,24},{4,4},{5,12},{6,20},{7,28},{8,1},{9,9},{... | collective-permute-start | bytes 786440 | tf_op jit(solution)/shard_map/ppermute | solution.py:415
  311.2 31.6 %collective-permute-start.123 = (f32[1,2,128,128]{3,2,1,0:T(8,128)S(1)}, f32[1,2,128,128]{3,2,1,0:T(8,128)S(1)}, u32[]{:S(2)}, u32[]{:S(2)}) collective-permute-start(f32[1,2,128,128]{3,2,1,0:T(8,128)S(1)} %get-tuple-element.383), channel_id=1, source_target_pairs={{0,24},{1,16},{2,8},{3,0},{4,28},{5,20},{6,12},{7,4},{8,25},{9,17}... | collective-permute-start | bytes 393224 | tf_op jit(solution)/shard_map/ppermute | solution.py:415
  314.9 27.2 %collective-permute-start.122 = (f32[1,2,128,128]{3,2,1,0:T(8,128)S(1)}, f32[1,2,128,128]{3,2,1,0:T(8,128)S(1)}, u32[]{:S(2)}, u32[]{:S(2)}) collective-permute-start(f32[1,2,128,128]{3,2,1,0:T(8,128)S(1)} %get-tuple-element.384), channel_id=1, source_target_pairs={{0,16},{1,24},{2,0},{3,8},{4,20},{5,28},{6,4},{7,12},{8,17},{9,25}... | collective-permute-start | bytes 393224 | tf_op jit(solution)/shard_map/ppermute | solution.py:415
  317.3 23.6 %collective-permute-start.121 = (f32[1,2,128,128]{3,2,1,0:T(8,128)S(1)}, f32[1,2,128,128]{3,2,1,0:T(8,128)S(1)}, u32[]{:S(2)}, u32[]{:S(2)}) collective-permute-start(f32[1,2,128,128]{3,2,1,0:T(8,128)S(1)} %get-tuple-element.385), channel_id=1, source_target_pairs={{0,8},{1,0},{2,24},{3,16},{4,12},{5,4},{6,28},{7,20},{8,9},{9,1},{... | collective-permute-start | bytes 393224 | tf_op jit(solution)/shard_map/ppermute | solution.py:415
  329.0 18.1 %collective-permute-start.134 = (f32[1,2,128,128]{3,2,1,0:T(8,128)S(1)}, f32[1,2,128,128]{3,2,1,0:T(8,128)S(1)}, u32[]{:S(2)}, u32[]{:S(2)}) collective-permute-start(f32[1,2,128,128]{3,2,1,0:T(8,128)S(1)} %get-tuple-element.350), channel_id=1, source_target_pairs={{0,24},{1,16},{2,8},{3,0},{4,28},{5,20},{6,12},{7,4},{8,25},{9,17}... | collective-permute-start | bytes 393224 | tf_op jit(solution)/shard_map/ppermute | solution.py:415
  329.5 17.6 %collective-permute-start.133 = (f32[1,2,128,128]{3,2,1,0:T(8,128)S(1)}, f32[1,2,128,128]{3,2,1,0:T(8,128)S(1)}, u32[]{:S(2)}, u32[]{:S(2)}) collective-permute-start(f32[1,2,128,128]{3,2,1,0:T(8,128)S(1)} %get-tuple-element.349), channel_id=1, source_target_pairs={{0,16},{1,24},{2,0},{3,8},{4,20},{5,28},{6,4},{7,12},{8,17},{9,25}... | collective-permute-start | bytes 393224 | tf_op jit(solution)/shard_map/ppermute | solution.py:415
  (203 other events, 2851.5 us)
